TPU v7x, 512 devices: a whole 4x4x16 slice. The times are simulated.
512 devices in a mesh: dp: 32 (over z, core), member: 16 (over y, x).
Axes of the slice: x: 4, y: 4, z: 16, core: 2. Of those that a mesh axis runs over, the one named last changes fastest.
Arguments:
- tokens: bfloat16 [4096, 4096], P('dp', 'member'), may hold values from -6 to 6
- routes: int32 [4096, 2], P('dp'), may hold values from 0 to 7, all different within a row; in each aligned block of 128 rows (0 to 127, 128 to 255, ...) at most 34 rows name the same one
- route_weights: float32 [4096, 2], P('dp'), may hold values from 0.2 to 1
- up_stacked: bfloat16 [8, 4096, 7168], P(None, ('member', 'dp')), may hold values from -0.09375 to 0.09375
- down_stacked: bfloat16 [8, 4096, 7168], P(None, ('member', 'dp')), may hold values from -0.0625 to 0.0625
- cotangent: bfloat16 [4096, 4096], P('dp', 'member'), may hold values from -6 to 6
Outputs:
- mixed: bfloat16 [4096, 4096], P('dp', 'member')
- grad_tokens: bfloat16 [4096, 4096], P('dp', 'member')
- grad_up: bfloat16 [32, 4096, 1792], P('dp', 'member')
- grad_down: bfloat16 [32, 4096, 1792], P('dp', 'member')
Inputs may be any that keep to these rules, and one draw needn't show every extreme that they name: `routes`: each row names two different experts. In each aligned block of 128 rows no expert is named by more than 34 rows, and in some block some expert is named by exactly 34 rows.
All inputs are finite; a program needn't handle non-finite values.
Results may differ from a plain program's by a relative error of at most 0.018.
Values may be sent and summed in bfloat16 or wider, within the bound.
A program may use at most 64 MiB of HBM per device.

v0:
```python
import jax
import jax.numpy as jnp
from jax import lax
from jax.sharding import PartitionSpec as P

FF_W = 7168
E = 8
CAP = 34


def contract(left, right, left_dim, right_dim):
    return lax.dot_general(
        left, right, (((left_dim,), (right_dim,)), ((), ())), preferred_element_type=jnp.float32
    )


def body(tokens, routes, route_weights, up_stacked, down_stacked, cotangent):
    dp_count = lax.axis_size("dp")
    member_count = lax.axis_size("member")
    quarters = dp_count // E
    share_rows = up_stacked.shape[1]
    features = tokens.shape[1]
    hidden_own = FF_W // quarters
    per_member = hidden_own // member_count
    slots_all = E * CAP
    up_parts = (
        up_stacked.reshape(E, share_rows, quarters, hidden_own)
        .transpose(0, 2, 1, 3)
        .reshape(dp_count, share_rows, hidden_own)
    )
    down_parts = (
        down_stacked.reshape(E, share_rows, quarters, hidden_own)
        .transpose(0, 2, 1, 3)
        .reshape(dp_count, share_rows, hidden_own)
    )
    up_own, down_own = (
        lax.all_to_all(up_parts, "dp", split_axis=0, concat_axis=1, tiled=True),
        lax.all_to_all(down_parts, "dp", split_axis=0, concat_axis=1, tiled=True),
    )
    up_own = up_own.reshape(dp_count * share_rows, hidden_own)
    down_own = down_own.reshape(dp_count * share_rows, hidden_own)
    chosen = (routes[:, :, None] == jnp.arange(E, dtype=jnp.int32)[None, None, :]).astype(jnp.int32)
    flat_hits = chosen.reshape(-1, E)
    before = jnp.cumsum(flat_hits, axis=0) - flat_hits
    slot_pos = jnp.sum(before * flat_hits, axis=1).reshape(-1, 2)
    target = routes * CAP + slot_pos
    slot_hits = jnp.arange(slots_all, dtype=jnp.int32)[:, None, None] == target[None, :, :]
    pick_table = jnp.sum(slot_hits.astype(jnp.float32), axis=2)
    weighted = jnp.sum(jnp.where(slot_hits, route_weights[None, :, :], 0.0), axis=2)
    x_local = jnp.dot(
        pick_table.astype(jnp.bfloat16), tokens, preferred_element_type=jnp.float32
    ).astype(jnp.bfloat16)
    d_local = jnp.dot(
        weighted, cotangent.astype(jnp.float32), precision=lax.Precision.HIGHEST
    ).astype(jnp.bfloat16)

    def spread(local):
        return jnp.broadcast_to(
            local.reshape(E, 1, CAP, features), (E, quarters, CAP, features)
        ).reshape(dp_count, CAP, features)

    def collect(returned):
        return jnp.sum(returned.reshape(E, quarters, CAP, features), axis=1).reshape(
            slots_all, features
        )

    x_in = lax.all_to_all(spread(x_local), "dp", split_axis=0, concat_axis=0, tiled=True).reshape(
        dp_count * CAP, features
    )
    partial_value = jnp.dot(x_in, up_own, preferred_element_type=jnp.float32).astype(jnp.bfloat16)
    pre_full = lax.psum(partial_value, "member").astype(jnp.float32)
    act_full = jax.nn.silu(pre_full).astype(jnp.bfloat16)
    y_part = contract(act_full, down_own, 1, 1)
    y_part, pre_full, act_full = (y_part, pre_full, act_full)
    y_back = lax.all_to_all(
        y_part.reshape(dp_count, CAP, features).astype(jnp.bfloat16),
        "dp",
        split_axis=0,
        concat_axis=0,
        tiled=True,
    ).astype(jnp.float32)
    d_in = lax.all_to_all(spread(d_local), "dp", split_axis=0, concat_axis=0, tiled=True).reshape(
        dp_count * CAP, features
    )
    d_act = lax.psum_scatter(
        contract(down_own, d_in, 0, 1).astype(jnp.bfloat16),
        "member",
        scatter_dimension=0,
        tiled=True,
    ).astype(jnp.float32)
    own_start = lax.axis_index("member") * per_member
    pre_share = lax.dynamic_slice_in_dim(pre_full, own_start, per_member, 1).T
    sigma = jax.nn.sigmoid(pre_share)
    d_share = (d_act * sigma * (1.0 + pre_share * (1.0 - sigma))).astype(jnp.bfloat16)
    d_pre = lax.all_gather(d_share, "member", axis=0, tiled=True)
    g_down = contract(d_in, act_full, 0, 0)
    g_up = contract(x_in, d_pre, 0, 1)
    dx_part = contract(d_pre, up_own, 0, 1)
    dx_part, g_up, g_down = (dx_part, g_up, g_down)
    dx_back = lax.all_to_all(
        dx_part.reshape(dp_count, CAP, features).astype(jnp.bfloat16),
        "dp",
        split_axis=0,
        concat_axis=0,
        tiled=True,
    ).astype(jnp.float32)
    y_slots = collect(y_back)
    dx_slots = collect(dx_back)
    mixed = jnp.dot(weighted.T, y_slots, precision=lax.Precision.HIGHEST).astype(jnp.bfloat16)
    grad_tokens = jnp.dot(pick_table.T, dx_slots, precision=lax.Precision.HIGHEST).astype(
        jnp.bfloat16
    )
    grad_up = g_up.astype(jnp.bfloat16).reshape(1, features, hidden_own)
    grad_down = g_down.astype(jnp.bfloat16).reshape(1, features, hidden_own)
    return (mixed, grad_tokens, grad_up, grad_down)


def solution(mesh):
    placed = (
        P("dp", "member"),
        P("dp", None),
        P("dp", None),
        P(None, ("member", "dp"), None),
        P(None, ("member", "dp"), None),
        P("dp", "member"),
    )
    return jax.shard_map(
        body,
        mesh=mesh,
        in_specs=placed,
        out_specs=(
            P("dp", "member"),
            P("dp", "member"),
            P("dp", "member", None),
            P("dp", "member", None),
        ),
        check_vma=False,
    )
```

profile of v0, /device:TPU:1, one launch (start us, length us, event | category | flops | bytes accessed | tf_op | source)
XLA Modules:
  0.0 533.8 jit_solution(7201500621114122409)
XLA Ops:
  7.2 0.0 copy-start
  7.2 0.8 copy.35
  8.0 0.1 eq.44
  8.1 0.1 eq.40
  8.3 0.6 reduce-window.6
  8.9 0.2 slice_reduce_fusion
  9.1 0.1 fusion.14
  9.2 0.1 reshape.98
  9.4 0.1 copy.37
  9.4 0.7 multiply_add_fusion
  10.1 0.8 convert_reduce_fusion.2
  10.9 0.0 copy-done
  10.9 0.3 convolution_convert_fusion.6
  11.2 0.9 broadcast_in_dim.36
  12.1 16.8 %all-to-all-start.4 = ((bf16[32,34,256]{2,1,0:T(8,128)(2,1)}), bf16[32,34,256]{2,1,0:T(8,128)(2,1)S(1)}, u32[]{:S(2)}, u32[]{:S(2)}) async-start(bf16[32,34,256]{2,1,0:T(8,128)(2,1)} %bitcast.9), calls=%async_computation.4 | async-start | bytes 1310720 | tf_op jit(solution)/shard_map/all_to_all | solution.py:82
  28.9 1.0 convolution_convert_fusion.7
  30.0 38.0 %all-to-all-done.4 = bf16[32,34,256]{2,1,0:T(8,128)(2,1)S(1)} async-done(((bf16[32,34,256]{2,1,0:T(8,128)(2,1)}), bf16[32,34,256]{2,1,0:T(8,128)(2,1)S(1)}, u32[]{:S(2)}, u32[]{:S(2)}) %all-to-all-start.4) | async-done | bytes 557088 | tf_op jit(solution)/shard_map/all_to_all | solution.py:82
  68.0 0.9 broadcast_in_dim.34
  68.8 4.1 all-to-all-start
  72.9 1.3 fusion.16
  74.3 1.0 pad_maximum_fusion.1
  75.3 36.7 %all-to-all-done = bf16[32,34,256]{2,1,0:T(8,128)(2,1)S(1)} async-done(((bf16[32,34,256]{2,1,0:T(8,128)(2,1)}), bf16[32,34,256]{2,1,0:T(8,128)(2,1)S(1)}, u32[]{:S(2)}, u32[]{:S(2)}) %all-to-all-start) | async-done | bytes 557088 | tf_op jit(solution)/shard_map/all_to_all | solution.py:67
  112.0 0.0 copy-start.2
  112.0 0.8 copy-done.2
  112.8 4.5 all-to-all-start.2
  117.3 1.3 fusion.17
  118.7 1.0 pad_maximum_fusion
  119.7 47.9 %all-to-all-done.2 = bf16[32,8,1792]{2,1,0:T(8,128)(2,1)S(1)} async-done(((bf16[32,8,1792]{2,1,0:T(8,128)(2,1)}), bf16[32,8,1792]{2,1,0:T(8,128)(2,1)S(1)}, u32[]{:S(2)}, u32[]{:S(2)}) %all-to-all-start.2) | async-done | bytes 917536 | tf_op jit(solution)/shard_map/all_to_all | solution.py:38
  167.6 4.5 all-to-all-start.1
  172.1 0.0 all-reduce.4.cloned.1.call-start
  172.2 1.0 reshape.109
  173.1 1.3 reshape.100
  174.4 4.4 convolution_convert_fusion
  178.8 6.4 %copy.38 = bf16[1792,1088]{0,1:T(8,128)(2,1)} copy(bf16[1792,1088]{1,0:T(8,128)(2,1)} %convolution_convert_fusion) | data formatting | bytes 7798784 | tf_op jit(solution)/shard_map/convert_element_type | solution.py:86
  185.2 37.2 %all-to-all-done.1 = bf16[32,8,1792]{2,1,0:T(8,128)(2,1)S(1)} async-done(((bf16[32,8,1792]{2,1,0:T(8,128)(2,1)}), bf16[32,8,1792]{2,1,0:T(8,128)(2,1)S(1)}, u32[]{:S(2)}, u32[]{:S(2)}) %all-to-all-start.1) | async-done | bytes 917536 | tf_op jit(solution)/shard_map/all_to_all | solution.py:37
  222.4 3.1 convolution_convert_fusion.1
  225.5 0.0 all-reduce.4.cloned.1.call-update
  225.5 0.0 all-gather.2.cloned.1.call-start
  225.6 1.3 dynamic-slice
  227.5 156.5 %all-reduce.4.cloned.1.call-done = (bf16[1088,1792]{1,0:T(8,128)(2,1)}, bf16[1792,1088]{0,1:T(8,128)(2,1)}) async-done(((bf16[1088,1792]{1,0:T(8,128)(2,1)}, bf16[1792,1088]{0,1:T(8,128)(2,1)}), (bf16[1088,1792]{1,0:T(8,128)(2,1)}, bf16[1792,1088]{0,1:T(8,128)(2,1)})) %all-reduce.4.cloned.1.call-update) | async-done | bytes 7798800 | tf_op jit(solution)/shard_map/psum | solution.py:71
  384.0 2.7 convert_element_type.65
  386.7 1.4 fusion.11
  388.1 0.9 copy.39
  389.0 0.0 all-gather.2.cloned.1.call-update
  389.0 5.0 multiply_convert_fusion
  394.0 6.9 %dot_general.38 = bf16[32,34,1792]{2,1,0:T(8,128)(2,1)} reshape(bf16[1088,1792]{1,0:T(8,128)(2,1)} %multiply_convert_fusion) | data formatting | bytes 7798784 | tf_op jit(solution)/shard_map/dot_general | solution.py:12
  400.9 4.6 convolution_convert_fusion.5
  405.5 13.0 %all-to-all-start.3 = ((bf16[32,34,256]{2,1,0:T(8,128)(2,1)}), bf16[32,34,256]{2,1,0:T(8,128)(2,1)S(1)}, u32[]{:S(2)}, u32[]{:S(2)}) async-start(bf16[32,34,256]{2,1,0:T(8,128)(2,1)} %convolution_convert_fusion.5), calls=%async_computation.3 | async-start | bytes 1310720 | tf_op jit(solution)/shard_map/all_to_all | solution.py:75
  418.5 37.1 %all-gather.2.cloned.1.call-done = bf16[1792,1088]{1,0:T(8,128)(2,1)} async-done(((bf16[112,1088]{1,0:T(8,128)(2,1)}), bf16[1792,1088]{1,0:T(8,128)(2,1)}) %all-gather.2.cloned.1.call-update) | async-done | bytes 3899408 | tf_op jit(solution)/shard_map/all_gather | solution.py:95
  455.6 6.4 %copy.40 = bf16[1088,1792]{1,0:T(8,128)(2,1)} copy(bf16[1088,1792]{0,1:T(8,128)(2,1)} %bitcast.72) | data formatting | bytes 7798784 | tf_op jit(solution)/shard_map/dot_general | solution.py:12
  462.0 6.9 %dot_general.44 = bf16[32,34,1792]{2,1,0:T(8,128)(2,1)} reshape(bf16[1088,1792]{1,0:T(8,128)(2,1)} %copy.40) | data formatting | bytes 7798784 | tf_op jit(solution)/shard_map/dot_general | solution.py:12
  468.9 4.7 convolution_convert_fusion.4
  473.6 0.0 all-to-all-done.3
  473.6 13.0 %all-to-all-start.5 = ((bf16[32,34,256]{2,1,0:T(8,128)(2,1)}), bf16[32,34,256]{2,1,0:T(8,128)(2,1)S(1)}, u32[]{:S(2)}, u32[]{:S(2)}) async-start(bf16[32,34,256]{2,1,0:T(8,128)(2,1)} %convolution_convert_fusion.4), calls=%async_computation.5 | async-start | bytes 1310720 | tf_op jit(solution)/shard_map/all_to_all | solution.py:100
  486.6 0.0 copy-done.3
  486.6 4.4 fusion.1
  491.0 0.1 convert_reduce_fusion.1
  491.2 0.0 copy-start.1
  491.2 1.1 convolution_convert_fusion.9
  492.3 4.5 fusion
  496.8 28.9 %all-to-all-done.5 = bf16[32,34,256]{2,1,0:T(8,128)(2,1)S(1)} async-done(((bf16[32,34,256]{2,1,0:T(8,128)(2,1)}), bf16[32,34,256]{2,1,0:T(8,128)(2,1)S(1)}, u32[]{:S(2)}, u32[]{:S(2)}) %all-to-all-start.5) | async-done | bytes 557088 | tf_op jit(solution)/shard_map/all_to_all | solution.py:100
  525.7 0.1 convert_reduce_fusion
  525.8 1.1 convolution_convert_fusion.8
  527.0 0.0 copy-done.1
  (8 shorter events, 0.2 us)
Async XLA Ops:
  7.2 3.7 copy-start
  12.1 55.9 %all-to-all-start.4 = ((bf16[32,34,256]{2,1,0:T(8,128)(2,1)}), bf16[32,34,256]{2,1,0:T(8,128)(2,1)S(1)}, u32[]{:S(2)}, u32[]{:S(2)}) async-start(bf16[32,34,256]{2,1,0:T(8,128)(2,1)} %bitcast.9), calls=%async_computation.4 | async-start | bytes 1310720 | tf_op jit(solution)/shard_map/all_to_all | solution.py:82
  68.8 43.1 %all-to-all-start = ((bf16[32,34,256]{2,1,0:T(8,128)(2,1)}), bf16[32,34,256]{2,1,0:T(8,128)(2,1)S(1)}, u32[]{:S(2)}, u32[]{:S(2)}) async-start(bf16[32,34,256]{2,1,0:T(8,128)(2,1)} %bitcast.2), calls=%async_computation | async-start | bytes 1310720 | tf_op jit(solution)/shard_map/all_to_all | solution.py:67
  112.0 0.8 copy-start.2
  112.8 54.7 %all-to-all-start.2 = ((bf16[32,8,1792]{2,1,0:T(8,128)(2,1)}), bf16[32,8,1792]{2,1,0:T(8,128)(2,1)S(1)}, u32[]{:S(2)}, u32[]{:S(2)}) async-start(bf16[32,8,1792]{2,1,0:T(8,128)(2,1)} %bitcast.5), calls=%async_computation.2 | async-start | bytes 1835008 | tf_op jit(solution)/shard_map/all_to_all | solution.py:38
  167.6 54.8 %all-to-all-start.1 = ((bf16[32,8,1792]{2,1,0:T(8,128)(2,1)}), bf16[32,8,1792]{2,1,0:T(8,128)(2,1)S(1)}, u32[]{:S(2)}, u32[]{:S(2)}) async-start(bf16[32,8,1792]{2,1,0:T(8,128)(2,1)} %bitcast.3), calls=%async_computation.1 | async-start | bytes 1835008 | tf_op jit(solution)/shard_map/all_to_all | solution.py:37
  172.1 211.8 %all-reduce.4.cloned.1.call-start = ((), (), s32[]{:S(2)}) async-start(), calls=%async_computation.7 | async-start | bytes 15597568 | tf_op jit(solution)/shard_map/psum | solution.py:71
  225.5 230.1 %all-gather.2.cloned.1.call-start = ((), (), s32[]{:S(2)}) async-start(), calls=%async_computation.6 | async-start | bytes 4386816 | tf_op jit(solution)/shard_map/all_gather | solution.py:95
  405.5 68.1 %all-to-all-start.3 = ((bf16[32,34,256]{2,1,0:T(8,128)(2,1)}), bf16[32,34,256]{2,1,0:T(8,128)(2,1)S(1)}, u32[]{:S(2)}, u32[]{:S(2)}) async-start(bf16[32,34,256]{2,1,0:T(8,128)(2,1)} %convolution_convert_fusion.5), calls=%async_computation.3 | async-start | bytes 1310720 | tf_op jit(solution)/shard_map/all_to_all | solution.py:75
  468.9 17.7 %copy-start.3 = (bf16[1088,256]{1,0:T(8,128)(2,1)S(1)}, bf16[1088,256]{1,0:T(8,128)(2,1)}, u32[]{:S(2)}) copy-start(bf16[1088,256]{1,0:T(8,128)(2,1)} %reshape.109) | copy-start | bytes 1671172
  473.6 52.1 %all-to-all-start.5 = ((bf16[32,34,256]{2,1,0:T(8,128)(2,1)}), bf16[32,34,256]{2,1,0:T(8,128)(2,1)S(1)}, u32[]{:S(2)}, u32[]{:S(2)}) async-start(bf16[32,34,256]{2,1,0:T(8,128)(2,1)} %convolution_convert_fusion.4), calls=%async_computation.5 | async-start | bytes 1310720 | tf_op jit(solution)/shard_map/all_to_all | solution.py:100
  491.2 35.8 %copy-start.1 = (bf16[128,256]{1,0:T(8,128)(2,1)S(1)}, bf16[128,256]{1,0:T(8,128)(2,1)}, u32[]{:S(2)}) copy-start(bf16[128,256]{1,0:T(8,128)(2,1)} %param.11) | copy-start | bytes 196612
Sparse Core Ops, SparseCore 0:
  225.7 158.2 all-reduce.3
  389.1 66.4 all-gather.1
where the time goes:
time: 535 us; the launch traced here: 534 us
  waiting for transfers between devices  382 us (71%)
  starting transfers between devices  55.9 us (10%)
  local copies, waits for them, and re-layouts  38 us (7%)
  matrix products  29.2 us (5%)
  between operations  14.9 us (3%)
  other arithmetic  13.5 us (3%)
    psum x1, waiting for transfers between devices, body(): pre_full = lax.psum(partial_value, 'member').astype(jnp.float32)  156 us
    all_to_all x1, waiting for transfers between devices, body(): lax.all_to_all(down_parts, 'dp', split_axis=0, concat_axis=1, tiled=True)  47.9 us
    all_to_all x1, waiting for transfers between devices, body(): lax.all_to_all(spread(d_local), 'dp', split_axis=0, concat_axis=0, tiled=...  38 us
    all_to_all x1, waiting for transfers between devices, body(): lax.all_to_all(up_parts, 'dp', split_axis=0, concat_axis=1, tiled=True)  37.2 us
    all_gather x1, waiting for transfers between devices, body(): d_pre = lax.all_gather(d_share, 'member', axis=0, tiled=True)  37.1 us
    all_to_all x1, waiting for transfers between devices, body(): lax.all_to_all(spread(x_local), 'dp', split_axis=0, concat_axis=0, tiled=...  36.7 us
    all_to_all x1, waiting for transfers between devices, body(): lax.all_to_all(dx_part.reshape(dp_count, CAP, features).astype(jnp.bfloat...  28.9 us
    dot_general x5, matrix products, contract(): lax.dot_general(left, right, (((left_dim,), (right_dim,)), ((), ())), pre...  22.5 us
  transfers between devices with their start and end apart: 8, of which 7 were waited for; matrix products, arithmetic and copies ran while one was open for 12% of the time, Pallas kernels for 0%

commit v1 on v0

--- a/solution.py
+++ b/solution.py
@@ -39,10 +39,23 @@
     )
     up_own = up_own.reshape(dp_count * share_rows, hidden_own)
     down_own = down_own.reshape(dp_count * share_rows, hidden_own)
-    chosen = (routes[:, :, None] == jnp.arange(E, dtype=jnp.int32)[None, None, :]).astype(jnp.int32)
-    flat_hits = chosen.reshape(-1, E)
-    before = jnp.cumsum(flat_hits, axis=0) - flat_hits
-    slot_pos = jnp.sum(before * flat_hits, axis=1).reshape(-1, 2)
+    chosen = jnp.sum(
+        (routes[:, :, None] == jnp.arange(E, dtype=jnp.int32)[None, None, :]).astype(jnp.float32),
+        axis=1,
+    )
+    rows = jnp.arange(routes.shape[0], dtype=jnp.int32)
+    earlier = (rows[None, :] < rows[:, None]).astype(jnp.bfloat16)
+    before = jnp.dot(
+        earlier, chosen.astype(jnp.bfloat16), preferred_element_type=jnp.float32
+    ).astype(jnp.int32)
+    slot_pos = jnp.sum(
+        jnp.where(
+            routes[:, :, None] == jnp.arange(E, dtype=jnp.int32)[None, None, :],
+            before[:, None, :],
+            0,
+        ),
+        axis=2,
+    )
     target = routes * CAP + slot_pos
     slot_hits = jnp.arange(slots_all, dtype=jnp.int32)[:, None, None] == target[None, :, :]
     pick_table = jnp.sum(slot_hits.astype(jnp.float32), axis=2)

time: 535 us -> 535 us (level)
  no operation moved by 1% of the time
where the time goes in v1:
time: 535 us; the launch traced here: 533 us
  waiting for transfers between devices  382 us (71%)
  starting transfers between devices  55.9 us (10%)
  local copies, waits for them, and re-layouts  36.6 us (7%)
  matrix products  29.3 us (5%)
  between operations  14.9 us (3%)
  other arithmetic  14.2 us (3%)
    psum x1, waiting for transfers between devices, body(): pre_full = lax.psum(partial_value, 'member').astype(jnp.float32)  156 us
    all_to_all x1, waiting for transfers between devices, body(): lax.all_to_all(down_parts, 'dp', split_axis=0, concat_axis=1, tiled=True)  47.9 us
    all_to_all x1, waiting for transfers between devices, body(): lax.all_to_all(spread(d_local), 'dp', split_axis=0, concat_axis=0, tiled=...  38 us
    all_to_all x1, waiting for transfers between devices, body(): lax.all_to_all(up_parts, 'dp', split_axis=0, concat_axis=1, tiled=True)  37.2 us
    all_gather x1, waiting for transfers between devices, body(): d_pre = lax.all_gather(d_share, 'member', axis=0, tiled=True)  37 us
    all_to_all x1, waiting for transfers between devices, body(): lax.all_to_all(spread(x_local), 'dp', split_axis=0, concat_axis=0, tiled=...  36.7 us
    all_to_all x1, waiting for transfers between devices, body(): lax.all_to_all(dx_part.reshape(dp_count, CAP, features).astype(jnp.bfloat...  28.9 us
    dot_general x5, matrix products, contract(): lax.dot_general(left, right, (((left_dim,), (right_dim,)), ((), ())), pre...  22.5 us
  transfers between devices with their start and end apart: 8, of which 7 were waited for; matrix products, arithmetic and copies ran while one was open for 12% of the time, Pallas kernels for 0%

profile of v1, /device:TPU:1, one launch (start us, length us, event | category | flops | bytes accessed | tf_op | source)
XLA Modules:
  0.0 533.1 jit_solution(2647584153746447925)
XLA Ops:
  7.2 0.0 copy-start
  7.2 0.7 convert_reduce_fusion.3
  7.9 0.1 convolution_convert_fusion.10
  8.0 0.7 select_reduce_fusion.1
  8.8 0.7 multiply_add_fusion
  9.4 0.8 convert_reduce_fusion.2
  10.2 0.0 copy-done
  10.2 0.3 convolution_convert_fusion.6
  10.5 0.9 broadcast_in_dim.55
  11.4 16.7 %all-to-all-start.4 = ((bf16[32,34,256]{2,1,0:T(8,128)(2,1)}), bf16[32,34,256]{2,1,0:T(8,128)(2,1)S(1)}, u32[]{:S(2)}, u32[]{:S(2)}) async-start(bf16[32,34,256]{2,1,0:T(8,128)(2,1)} %bitcast.7), calls=%async_computation.4 | async-start | bytes 1310720 | tf_op jit(solution)/shard_map/all_to_all | solution.py:95
  28.2 1.0 convolution_convert_fusion.7
  29.2 38.0 %all-to-all-done.4 = bf16[32,34,256]{2,1,0:T(8,128)(2,1)S(1)} async-done(((bf16[32,34,256]{2,1,0:T(8,128)(2,1)}), bf16[32,34,256]{2,1,0:T(8,128)(2,1)S(1)}, u32[]{:S(2)}, u32[]{:S(2)}) %all-to-all-start.4) | async-done | bytes 557088 | tf_op jit(solution)/shard_map/all_to_all | solution.py:95
  67.3 0.9 broadcast_in_dim.53
  68.1 4.1 all-to-all-start
  72.2 1.3 fusion.14
  73.6 1.0 pad_maximum_fusion.1
  74.6 36.7 %all-to-all-done = bf16[32,34,256]{2,1,0:T(8,128)(2,1)S(1)} async-done(((bf16[32,34,256]{2,1,0:T(8,128)(2,1)}), bf16[32,34,256]{2,1,0:T(8,128)(2,1)S(1)}, u32[]{:S(2)}, u32[]{:S(2)}) %all-to-all-start) | async-done | bytes 557088 | tf_op jit(solution)/shard_map/all_to_all | solution.py:80
  111.3 0.0 copy-start.2
  111.3 0.8 copy-done.2
  112.1 4.5 all-to-all-start.2
  116.6 1.3 fusion.15
  117.9 1.0 pad_maximum_fusion
  118.9 47.9 %all-to-all-done.2 = bf16[32,8,1792]{2,1,0:T(8,128)(2,1)S(1)} async-done(((bf16[32,8,1792]{2,1,0:T(8,128)(2,1)}), bf16[32,8,1792]{2,1,0:T(8,128)(2,1)S(1)}, u32[]{:S(2)}, u32[]{:S(2)}) %all-to-all-start.2) | async-done | bytes 917536 | tf_op jit(solution)/shard_map/all_to_all | solution.py:38
  166.9 4.5 all-to-all-start.1
  171.4 0.0 all-reduce.4.cloned.1.call-start
  171.5 1.0 reshape.88
  172.4 1.3 reshape.79
  173.7 4.4 convolution_convert_fusion
  178.1 6.4 %copy.27 = bf16[1792,1088]{0,1:T(8,128)(2,1)} copy(bf16[1792,1088]{1,0:T(8,128)(2,1)} %convolution_convert_fusion) | data formatting | bytes 7798784 | tf_op jit(solution)/shard_map/convert_element_type | solution.py:99
  184.5 37.2 %all-to-all-done.1 = bf16[32,8,1792]{2,1,0:T(8,128)(2,1)S(1)} async-done(((bf16[32,8,1792]{2,1,0:T(8,128)(2,1)}), bf16[32,8,1792]{2,1,0:T(8,128)(2,1)S(1)}, u32[]{:S(2)}, u32[]{:S(2)}) %all-to-all-start.1) | async-done | bytes 917536 | tf_op jit(solution)/shard_map/all_to_all | solution.py:37
  221.7 3.1 convolution_convert_fusion.1
  224.8 0.0 all-reduce.4.cloned.1.call-update
  224.8 0.0 all-gather.2.cloned.1.call-start
  224.9 1.3 dynamic-slice
  226.8 156.5 %all-reduce.4.cloned.1.call-done = (bf16[1088,1792]{1,0:T(8,128)(2,1)}, bf16[1792,1088]{0,1:T(8,128)(2,1)}) async-done(((bf16[1088,1792]{1,0:T(8,128)(2,1)}, bf16[1792,1088]{0,1:T(8,128)(2,1)}), (bf16[1088,1792]{1,0:T(8,128)(2,1)}, bf16[1792,1088]{0,1:T(8,128)(2,1)})) %all-reduce.4.cloned.1.call-update) | async-done | bytes 7798800 | tf_op jit(solution)/shard_map/psum | solution.py:84
  383.3 2.7 convert_element_type.68
  385.9 1.4 fusion.11
  387.4 0.9 copy.28
  388.2 0.0 all-gather.2.cloned.1.call-update
  388.3 5.0 multiply_convert_fusion
  393.3 6.9 %dot_general.42 = bf16[32,34,1792]{2,1,0:T(8,128)(2,1)} reshape(bf16[1088,1792]{1,0:T(8,128)(2,1)} %multiply_convert_fusion) | data formatting | bytes 7798784 | tf_op jit(solution)/shard_map/dot_general | solution.py:12
  400.3 4.6 convolution_convert_fusion.5
  404.8 13.0 %all-to-all-start.3 = ((bf16[32,34,256]{2,1,0:T(8,128)(2,1)}), bf16[32,34,256]{2,1,0:T(8,128)(2,1)S(1)}, u32[]{:S(2)}, u32[]{:S(2)}) async-start(bf16[32,34,256]{2,1,0:T(8,128)(2,1)} %convolution_convert_fusion.5), calls=%async_computation.3 | async-start | bytes 1310720 | tf_op jit(solution)/shard_map/all_to_all | solution.py:88
  417.9 37.0 %all-gather.2.cloned.1.call-done = bf16[1792,1088]{1,0:T(8,128)(2,1)} async-done(((bf16[112,1088]{1,0:T(8,128)(2,1)}), bf16[1792,1088]{1,0:T(8,128)(2,1)}) %all-gather.2.cloned.1.call-update) | async-done | bytes 3899408 | tf_op jit(solution)/shard_map/all_gather | solution.py:108
  454.9 6.4 %copy.29 = bf16[1088,1792]{1,0:T(8,128)(2,1)} copy(bf16[1088,1792]{0,1:T(8,128)(2,1)} %bitcast.65) | data formatting | bytes 7798784 | tf_op jit(solution)/shard_map/dot_general | solution.py:12
  461.3 6.9 %dot_general.48 = bf16[32,34,1792]{2,1,0:T(8,128)(2,1)} reshape(bf16[1088,1792]{1,0:T(8,128)(2,1)} %copy.29) | data formatting | bytes 7798784 | tf_op jit(solution)/shard_map/dot_general | solution.py:12
  468.2 0.0 copy-start.3
  468.2 4.7 convolution_convert_fusion.4
  472.9 0.0 all-to-all-done.3
  472.9 13.0 %all-to-all-start.5 = ((bf16[32,34,256]{2,1,0:T(8,128)(2,1)}), bf16[32,34,256]{2,1,0:T(8,128)(2,1)S(1)}, u32[]{:S(2)}, u32[]{:S(2)}) async-start(bf16[32,34,256]{2,1,0:T(8,128)(2,1)} %convolution_convert_fusion.4), calls=%async_computation.5 | async-start | bytes 1310720 | tf_op jit(solution)/shard_map/all_to_all | solution.py:113
  485.9 0.0 copy-done.3
  485.9 4.4 fusion.1
  490.4 0.1 convert_reduce_fusion.1
  490.5 0.0 copy-start.1
  490.5 1.1 convolution_convert_fusion.9
  491.6 4.5 fusion
  496.2 28.9 %all-to-all-done.5 = bf16[32,34,256]{2,1,0:T(8,128)(2,1)S(1)} async-done(((bf16[32,34,256]{2,1,0:T(8,128)(2,1)}), bf16[32,34,256]{2,1,0:T(8,128)(2,1)S(1)}, u32[]{:S(2)}, u32[]{:S(2)}) %all-to-all-start.5) | async-done | bytes 557088 | tf_op jit(solution)/shard_map/all_to_all | solution.py:113
  525.0 0.1 convert_reduce_fusion
  525.2 1.1 convolution_convert_fusion.8
  526.3 0.0 copy-done.1
  (4 shorter events, 0.2 us)
Async XLA Ops:
  7.2 3.0 copy-start
  11.4 55.9 %all-to-all-start.4 = ((bf16[32,34,256]{2,1,0:T(8,128)(2,1)}), bf16[32,34,256]{2,1,0:T(8,128)(2,1)S(1)}, u32[]{:S(2)}, u32[]{:S(2)}) async-start(bf16[32,34,256]{2,1,0:T(8,128)(2,1)} %bitcast.7), calls=%async_computation.4 | async-start | bytes 1310720 | tf_op jit(solution)/shard_map/all_to_all | solution.py:95
  68.1 43.1 %all-to-all-start = ((bf16[32,34,256]{2,1,0:T(8,128)(2,1)}), bf16[32,34,256]{2,1,0:T(8,128)(2,1)S(1)}, u32[]{:S(2)}, u32[]{:S(2)}) async-start(bf16[32,34,256]{2,1,0:T(8,128)(2,1)} %bitcast), calls=%async_computation | async-start | bytes 1310720 | tf_op jit(solution)/shard_map/all_to_all | solution.py:80
  111.3 0.8 copy-start.2
  112.1 54.7 %all-to-all-start.2 = ((bf16[32,8,1792]{2,1,0:T(8,128)(2,1)}), bf16[32,8,1792]{2,1,0:T(8,128)(2,1)S(1)}, u32[]{:S(2)}, u32[]{:S(2)}) async-start(bf16[32,8,1792]{2,1,0:T(8,128)(2,1)} %bitcast.3), calls=%async_computation.2 | async-start | bytes 1835008 | tf_op jit(solution)/shard_map/all_to_all | solution.py:38
  166.9 54.8 %all-to-all-start.1 = ((bf16[32,8,1792]{2,1,0:T(8,128)(2,1)}), bf16[32,8,1792]{2,1,0:T(8,128)(2,1)S(1)}, u32[]{:S(2)}, u32[]{:S(2)}) async-start(bf16[32,8,1792]{2,1,0:T(8,128)(2,1)} %bitcast.1), calls=%async_computation.1 | async-start | bytes 1835008 | tf_op jit(solution)/shard_map/all_to_all | solution.py:37
  171.4 211.8 %all-reduce.4.cloned.1.call-start = ((), (), s32[]{:S(2)}) async-start(), calls=%async_computation.7 | async-start | bytes 15597568 | tf_op jit(solution)/shard_map/psum | solution.py:84
  224.8 230.1 %all-gather.2.cloned.1.call-start = ((), (), s32[]{:S(2)}) async-start(), calls=%async_computation.6 | async-start | bytes 4386816 | tf_op jit(solution)/shard_map/all_gather | solution.py:108
  404.8 68.1 %all-to-all-start.3 = ((bf16[32,34,256]{2,1,0:T(8,128)(2,1)}), bf16[32,34,256]{2,1,0:T(8,128)(2,1)S(1)}, u32[]{:S(2)}, u32[]{:S(2)}) async-start(bf16[32,34,256]{2,1,0:T(8,128)(2,1)} %convolution_convert_fusion.5), calls=%async_computation.3 | async-start | bytes 1310720 | tf_op jit(solution)/shard_map/all_to_all | solution.py:88
  468.2 17.7 %copy-start.3 = (bf16[1088,256]{1,0:T(8,128)(2,1)S(1)}, bf16[1088,256]{1,0:T(8,128)(2,1)}, u32[]{:S(2)}) copy-start(bf16[1088,256]{1,0:T(8,128)(2,1)} %reshape.88) | copy-start | bytes 1671172
  472.9 52.1 %all-to-all-start.5 = ((bf16[32,34,256]{2,1,0:T(8,128)(2,1)}), bf16[32,34,256]{2,1,0:T(8,128)(2,1)S(1)}, u32[]{:S(2)}, u32[]{:S(2)}) async-start(bf16[32,34,256]{2,1,0:T(8,128)(2,1)} %convolution_convert_fusion.4), calls=%async_computation.5 | async-start | bytes 1310720 | tf_op jit(solution)/shard_map/all_to_all | solution.py:113
  490.5 35.8 %copy-start.1 = (bf16[128,256]{1,0:T(8,128)(2,1)S(1)}, bf16[128,256]{1,0:T(8,128)(2,1)}, u32[]{:S(2)}) copy-start(bf16[128,256]{1,0:T(8,128)(2,1)} %param.11) | copy-start | bytes 196612
Sparse Core Ops, SparseCore 0:
  224.9 158.2 all-reduce.3
  388.4 66.4 all-gather.1

commit v2 on v0

v2 whole, which is shorter than its diff:
```python
import jax
import jax.numpy as jnp
from jax import lax
from jax.experimental import pallas as pl
from jax.experimental.pallas import tpu as pltpu
from jax.sharding import PartitionSpec as P

FF_W = 7168
E = 8
CAP = 34
SIDE = 4
HEAD = 32
TAIL = 8
MSG = HEAD + TAIL
BF = jnp.bfloat16
F32 = jnp.float32


def dot(a, b, ca, cb):
    return lax.dot_general(a, b, (((ca,), (cb,)), ((), ())), preferred_element_type=F32)


def mult(i, n):
    return pl.multiple_of(i, n)


def layer_kernel(
    x_msg, d_msg, up, down,
    y_out, dx_out, gu_out, gd_out,
    up_own, down_own, x_got, d_got, y_msg, y_got, dx_msg, dx_got,
    xm, xt, dm, dt, tail32,
    pm, pt, r1m, r1t, sm, st, r2m, r2t, pre_m, pre_t, fm, ft,
    z_send, z_recv, o_send, o_recv, rs_send, rs_recv, ag_send, ag_recv,
):
    n_dp = lax.axis_size("dp")
    quarters = n_dp // E
    hid = up_own.shape[2]
    own_f = xm.shape[1]
    j = lax.axis_index("dp")
    m = lax.axis_index("member")
    cy, cx = m // SIDE, lax.rem(m, SIDE)
    half_rows = n_dp * HEAD // 2
    big = half_rows // SIDE
    small = big // SIDE
    t_rows = n_dp // 4 * TAIL
    ht = t_rows // 2
    wide = pt.shape[2] // SIDE
    narrow = wide // SIDE

    def first(h):
        return cx if h == 0 else cy

    def second(h):
        return cy if h == 0 else cx

    def peer_first(h, k):
        c = lax.rem(first(h) + k, SIDE)
        return c, {"member": cy * SIDE + c if h == 0 else c * SIDE + cx}

    def peer_second(h, k):
        c = lax.rem(second(h) + k, SIDE)
        return c, {"member": c * SIDE + cx if h == 0 else cy * SIDE + c}

    def shifted(i):
        step = i // 2 + 1
        return lax.rem(j + n_dp + step * (1 - 2 * lax.rem(i, 2)), n_dp)

    barrier = pltpu.get_barrier_semaphore()

    @pl.loop(0, n_dp - 1)
    def _(i):
        pl.semaphore_signal(barrier, inc=1, device_id={"dp": shifted(i)})

    for k in range(1, SIDE):
        pl.semaphore_signal(barrier, inc=1, device_id=peer_first(0, k)[1])
        pl.semaphore_signal(barrier, inc=1, device_id=peer_first(1, k)[1])
    pl.semaphore_wait(barrier, n_dp - 1 + 2 * (SIDE - 1))

    def weight_part(w, who):
        return w.at[who // quarters, :, pl.ds(mult(lax.rem(who, quarters) * hid, 128), hid)]

    def dispatch(n, msg, got, w, own):
        @pl.loop(0, n_dp - 1)
        def _(i):
            who = shifted(i)
            pltpu.make_async_remote_copy(
                src_ref=msg.at[who // quarters], dst_ref=got.at[j],
                send_sem=z_send.at[2 * n], recv_sem=z_recv.at[2 * n], device_id={"dp": who},
            ).start()

        pltpu.make_async_copy(msg.at[j // quarters], got.at[j], z_recv.at[2 * n]).start()

        @pl.loop(0, n_dp - 1)
        def _(i):
            who = shifted(i)
            pltpu.make_async_remote_copy(
                src_ref=weight_part(w, who), dst_ref=own.at[j],
                send_sem=z_send.at[2 * n + 1], recv_sem=z_recv.at[2 * n + 1], device_id={"dp": who},
            ).start()

        pltpu.make_async_copy(weight_part(w, j), own.at[j], z_recv.at[2 * n + 1]).start()

    def take(buf, sem):
        pltpu.make_async_copy(buf, buf, sem).wait()

    def sent(buf, sem):
        part = buf.at[pl.ds(0, n_dp - 1)]
        pltpu.make_async_copy(part, part, sem).wait()

    def gather_rows(got, main, tail):
        @pl.loop(0, n_dp)
        def _(s):
            main[pl.ds(mult(s * HEAD, HEAD), HEAD), :] = got[s, :HEAD, :]

        @pl.loop(0, n_dp // 4)
        def _(g):
            total = got[4 * g, HEAD:, :].astype(F32)
            for i in range(1, 4):
                total = total + got[4 * g + i, HEAD:, :].astype(F32)
            tail32[pl.ds(mult(g * TAIL, TAIL), TAIL), :] = total

        tail[...] = tail32[...].astype(BF)

    def partial(t, main, tail, own):
        @pl.loop(0, hid // 256)
        def _(c):
            cols = pl.ds(mult(c * 256, 256), 256)
            w = own[:, :, cols].reshape(own_f, 256)
            pm[t, :, cols] = dot(main[...], w, 1, 0).astype(BF)
            pt[t, :, cols] = dot(tail[...], w, 1, 0).astype(BF)

    def rs_copies(t, stage):
        out = []
        for h in range(2):
            for k in range(1, SIDE):
                if stage == 0:
                    c, dev = peer_first(h, k)
                    pairs = (
                        (pm.at[t, pl.ds(mult(h * half_rows + c * big, big), big), :], r1m.at[t, h, k - 1]),
                        (pt.at[t, pl.ds(h * ht, ht), pl.ds(mult(c * wide, wide), wide)], r1t.at[t, h, k - 1]),
                    )
                else:
                    c, dev = peer_second(h, k)
                    pairs = (
                        (sm.at[t, h, pl.ds(mult(c * small, small), small), :], r2m.at[t, h, k - 1]),
                        (st.at[t, h, :, pl.ds(mult(c * narrow, narrow), narrow)], r2t.at[t, h, k - 1]),
                    )
                for n, (src, dst) in enumerate(pairs):
                    out.append(
                        pltpu.make_async_remote_copy(
                            src_ref=src, dst_ref=dst,
                            send_sem=rs_send.at[t, stage, h, k - 1, n],
                            recv_sem=rs_recv.at[t, stage, h, k - 1, n], device_id=dev,
                        )
                    )
        return out

    def start(copies):
        for c in copies:
            c.start()
        return copies

    def arrived(copies):
        for c in copies:
            c.wait_recv()

    def left(copies):
        for c in copies:
            c.wait_send()

    def sum_first(t):
        for h in range(2):
            base = h * half_rows + first(h) * big

            @pl.loop(0, big // 16)
            def _(i):
                rows = pl.ds(mult(i * 16, 16), 16)
                total = pm[t, pl.ds(mult(base + i * 16, 16), 16), :].astype(F32)
                for k in range(SIDE - 1):
                    total = total + r1m[t, h, k, rows, :].astype(F32)
                sm[t, h, rows, :] = total.astype(BF)

            total = pt[t, pl.ds(h * ht, ht), pl.ds(mult(first(h) * wide, wide), wide)].astype(F32)
            for k in range(SIDE - 1):
                total = total + r1t[t, h, k].astype(F32)
            st[t, h] = total.astype(BF)

    def owned_rows(h):
        return pl.ds(mult(h * half_rows + first(h) * big + second(h) * small, small), small)

    def owned_cols(h):
        return pl.ds(mult(first(h) * wide + second(h) * narrow, narrow), narrow)

    def finish(t, fn):
        for h in range(2):

            @pl.loop(0, small // 16)
            def _(i):
                rows = pl.ds(mult(i * 16, 16), 16)
                total = sm[t, h, pl.ds(mult(second(h) * small + i * 16, 16), 16), :].astype(F32)
                for k in range(SIDE - 1):
                    total = total + r2m[t, h, k, rows, :].astype(F32)
                start_row = h * half_rows + first(h) * big + second(h) * small
                fm[t, pl.ds(mult(start_row + i * 16, 16), 16), :] = fn(total, pre_m.at[h, rows, :]).astype(BF)

            total = st[t, h, :, pl.ds(mult(second(h) * narrow, narrow), narrow)].astype(F32)
            for k in range(SIDE - 1):
                total = total + r2t[t, h, k].astype(F32)
            ft[t, pl.ds(h * ht, ht), owned_cols(h)] = fn(total, pre_t.at[h]).astype(BF)

    def silu(total, keep):
        keep[...] = total
        return total / (1.0 + jnp.exp(-total))

    def silu_back(total, keep):
        pre = keep[...]
        s = 1.0 / (1.0 + jnp.exp(-pre))
        return total * s * (1.0 + pre * (1.0 - s))

    def ag_copies(t, stage):
        out = []
        for h in range(2):
            if stage == 0:
                rows, cols = owned_rows(h), owned_cols(h)
            else:
                rows = pl.ds(mult(h * half_rows + first(h) * big, big), big)
                cols = pl.ds(mult(first(h) * wide, wide), wide)
            for k in range(1, SIDE):
                dev = (peer_second if stage == 0 else peer_first)(h, k)[1]
                for n, ref in enumerate((fm.at[t, rows, :], ft.at[t, pl.ds(h * ht, ht), cols])):
                    out.append(
                        pltpu.make_async_remote_copy(
                            src_ref=ref, dst_ref=ref,
                            send_sem=ag_send.at[t, stage, h, k - 1, n],
                            recv_sem=ag_recv.at[t, stage, h, k - 1, n], device_id=dev,
                        )
                    )
        return out

    def back(t, own, msg):
        flat = own[...].reshape(own_f, hid)

        @pl.loop(0, n_dp // 8)
        def _(b):
            part = dot(fm[t, pl.ds(mult(b * 8 * HEAD, 8 * HEAD), 8 * HEAD), :], flat, 1, 1).astype(BF)
            for i in range(8):
                msg[8 * b + i, :HEAD, :] = part[i * HEAD : (i + 1) * HEAD, :]

        tail32[...] = dot(ft[t, :, :hid], flat, 1, 1)

        @pl.loop(0, n_dp)
        def _(s):
            msg[s, HEAD:, :] = tail32[pl.ds(mult(s // 4 * TAIL, TAIL), TAIL), :].astype(BF)

    def give_back(t, msg, got):
        @pl.loop(0, n_dp - 1)
        def _(i):
            who = shifted(i)
            pltpu.make_async_remote_copy(
                src_ref=msg.at[who], dst_ref=got.at[j],
                send_sem=o_send.at[t], recv_sem=o_recv.at[t], device_id={"dp": who},
            ).start()

        pltpu.make_async_copy(msg.at[j], got.at[j], o_recv.at[t]).start()

    def collect(got, out):
        @pl.loop(0, E)
        def _(e):
            total = got[quarters * e].astype(F32)
            for q in range(1, quarters):
                total = total + got[quarters * e + q].astype(F32)
            out[e] = total

    def gradient(main, tail, t, out):
        left_m, left_t = main[...], tail[...]

        @pl.loop(0, hid // 256)
        def _(c):
            cols = pl.ds(mult(c * 256, 256), 256)
            g = dot(left_m, fm[t, :, cols], 0, 0) + dot(left_t, ft[t, :, cols], 0, 0)
            out[:, cols] = g.astype(BF)

    dispatch(0, x_msg, x_got, up, up_own)
    dispatch(1, d_msg, d_got, down, down_own)
    pt[:, :, hid:] = jnp.zeros((2, t_rows, pt.shape[2] - hid), BF)

    take(x_got, z_recv.at[0])
    gather_rows(x_got, xm, xt)
    take(up_own, z_recv.at[1])
    partial(0, xm, xt, up_own)
    rs00 = start(rs_copies(0, 0))
    arrived(rs00)
    sum_first(0)
    rs01 = start(rs_copies(0, 1))
    arrived(rs01)
    finish(0, silu)
    ag00 = start(ag_copies(0, 0))
    arrived(ag00)
    ag01 = start(ag_copies(0, 1))

    take(d_got, z_recv.at[2])
    gather_rows(d_got, dm, dt)
    take(down_own, z_recv.at[3])
    partial(1, dm, dt, down_own)
    rs10 = start(rs_copies(1, 0))
    arrived(ag01)
    back(0, down_own, y_msg)
    give_back(0, y_msg, y_got)
    arrived(rs10)
    sum_first(1)
    rs11 = start(rs_copies(1, 1))
    arrived(rs11)
    finish(1, silu_back)
    ag10 = start(ag_copies(1, 0))
    arrived(ag10)
    ag11 = start(ag_copies(1, 1))
    gradient(dm, dt, 0, gd_out)
    arrived(ag11)
    back(1, up_own, dx_msg)
    give_back(1, dx_msg, dx_got)
    gradient(xm, xt, 1, gu_out)
    take(y_got, o_recv.at[0])
    collect(y_got, y_out)
    take(dx_got, o_recv.at[1])
    collect(dx_got, dx_out)
    for copies in (rs00, rs01, ag00, ag01, rs10, rs11, ag10, ag11):
        left(copies)
    sent(x_got, z_send.at[0])
    sent(up_own, z_send.at[1])
    sent(d_got, z_send.at[2])
    sent(down_own, z_send.at[3])
    sent(y_got, o_send.at[0])
    sent(dx_got, o_send.at[1])


def layer(x_msg, d_msg, up, down):
    n_dp = lax.axis_size("dp")
    own_f = x_msg.shape[2]
    rows = up.shape[1]
    hid = up.shape[2] // (n_dp // E)
    main = n_dp * HEAD
    tails = n_dp // 4 * TAIL
    wide = -(-hid // (SIDE * SIDE * 128)) * SIDE * SIDE * 128
    big = main // 2 // SIDE
    small = big // SIDE
    ht = tails // 2
    vm = pltpu.VMEM
    dma = pltpu.SemaphoreType.DMA
    return pl.pallas_call(
        layer_kernel,
        name="layer",
        out_shape=(
            jax.ShapeDtypeStruct((E, MSG, own_f), F32),
            jax.ShapeDtypeStruct((E, MSG, own_f), F32),
            jax.ShapeDtypeStruct((own_f, hid), BF),
            jax.ShapeDtypeStruct((own_f, hid), BF),
        ),
        in_specs=[pl.BlockSpec(memory_space=pltpu.VMEM)] * 2 + [pl.BlockSpec(memory_space=pl.ANY)] * 2,
        out_specs=[pl.BlockSpec(memory_space=pltpu.VMEM)] * 4,
        scratch_shapes=[
            vm((n_dp, rows, hid), BF), vm((n_dp, rows, hid), BF),
            vm((n_dp, MSG, own_f), BF), vm((n_dp, MSG, own_f), BF),
            vm((n_dp, MSG, own_f), BF), vm((n_dp, MSG, own_f), BF),
            vm((n_dp, MSG, own_f), BF), vm((n_dp, MSG, own_f), BF),
            vm((main, own_f), BF), vm((tails, own_f), BF),
            vm((main, own_f), BF), vm((tails, own_f), BF),
            vm((tails, own_f), F32),
            vm((2, main, hid), BF), vm((2, tails, wide), BF),
            vm((2, 2, SIDE - 1, big, hid), BF), vm((2, 2, SIDE - 1, ht, wide // SIDE), BF),
            vm((2, 2, big, hid), BF), vm((2, 2, ht, wide // SIDE), BF),
            vm((2, 2, SIDE - 1, small, hid), BF), vm((2, 2, SIDE - 1, ht, wide // SIDE // SIDE), BF),
            vm((2, small, hid), F32), vm((2, ht, wide // SIDE // SIDE), F32),
            vm((2, main, hid), BF), vm((2, tails, wide), BF),
            dma((4,)), dma((4,)), dma((2,)), dma((2,)),
            dma((2, 2, 2, SIDE - 1, 2)), dma((2, 2, 2, SIDE - 1, 2)),
            dma((2, 2, 2, SIDE - 1, 2)), dma((2, 2, 2, SIDE - 1, 2)),
        ],
        compiler_params=pltpu.CompilerParams(
            collective_id=0, has_side_effects=True, vmem_limit_bytes=58 * 2**20
        ),
    )(x_msg, d_msg, up, down)


def body(tokens, routes, route_weights, up_stacked, down_stacked, cotangent):
    experts = jnp.arange(E, dtype=jnp.int32)
    named = routes[:, :, None] == experts[None, None, :]
    chosen = jnp.sum(named.astype(F32), axis=1)
    rows = jnp.arange(routes.shape[0], dtype=jnp.int32)
    earlier = (rows[None, :] < rows[:, None]).astype(BF)
    before = jnp.dot(earlier, chosen.astype(BF), preferred_element_type=F32).astype(jnp.int32)
    slot_pos = jnp.sum(jnp.where(named, before[:, None, :], 0), axis=2)
    shift = 2 * lax.rem(lax.axis_index("dp"), 4)
    target = routes * MSG + slot_pos + jnp.where(slot_pos >= HEAD, shift, 0)
    slot_hits = jnp.arange(E * MSG, dtype=jnp.int32)[:, None, None] == target[None, :, :]
    pick_table = jnp.sum(slot_hits.astype(F32), axis=2)
    weighted = jnp.sum(jnp.where(slot_hits, route_weights[None, :, :], 0.0), axis=2)
    features = tokens.shape[1]
    x_msg = jnp.dot(pick_table.astype(BF), tokens, preferred_element_type=F32).astype(BF)
    d_msg = jnp.dot(weighted, cotangent.astype(F32), precision=lax.Precision.HIGHEST).astype(BF)
    y_slots, dx_slots, g_up, g_down = layer(
        x_msg.reshape(E, MSG, features), d_msg.reshape(E, MSG, features), up_stacked, down_stacked
    )
    y_slots = y_slots.reshape(E * MSG, features)
    dx_slots = dx_slots.reshape(E * MSG, features)
    mixed = jnp.dot(weighted.T, y_slots, precision=lax.Precision.HIGHEST).astype(BF)
    grad_tokens = jnp.dot(pick_table.T, dx_slots, precision=lax.Precision.HIGHEST).astype(BF)
    return (mixed, grad_tokens, g_up[None], g_down[None])


def solution(mesh):
    placed = (
        P("dp", "member"),
        P("dp", None),
        P("dp", None),
        P(None, ("member", "dp"), None),
        P(None, ("member", "dp"), None),
        P("dp", "member"),
    )
    return jax.shard_map(
        body,
        mesh=mesh,
        in_specs=placed,
        out_specs=(
            P("dp", "member"),
            P("dp", "member"),
            P("dp", "member", None),
            P("dp", "member", None),
        ),
        check_vma=False,
    )
```

time: 535 us -> 272 us (0.51)
  the two profiles are of different devices: /device:TPU:1 before, /device:TPU:32 now
where the time goes in v2:
time: 272 us; the launch traced here: 271 us
  Pallas kernels  261 us (96%)
  matrix products  6.22 us (2%)
  local copies, waits for them, and re-layouts  3.82 us (1%)
    pallas_call x1, Pallas kernels, layer(): pl.pallas_call(layer_kernel, name='layer', out_shape=(jax.ShapeDtypeStruc...  261 us

profile of v2, /device:TPU:32, one launch (start us, length us, event | category | flops | bytes accessed | tf_op | source)
XLA Modules:
  0.0 271.5 jit_solution(12922377344842684333)
XLA Ops:
  0.6 0.0 copy-start
  0.7 0.0 copy-start.4
  0.7 0.7 copy-done.4
  1.4 0.1 convolution_convert_fusion.4
  1.5 0.0 copy-start.5
  1.6 0.7 copy-done.5
  2.2 0.1 convert_reduce_fusion
  2.3 0.0 copy-done
  2.3 0.0 copy-start.3
  2.3 0.9 convolution_convert_fusion.1
  3.2 0.0 copy-done.3
  3.2 0.9 convolution_convert_fusion
  4.1 260.6 %layer.1 = (f32[8,40,256]{2,1,0:T(8,128)}, f32[8,40,256]{2,1,0:T(8,128)}, bf16[256,1792]{1,0:T(8,128)(2,1)}, bf16[256,1792]{1,0:T(8,128)(2,1)}) custom-call(bf16[8,40,256]{2,1,0:T(8,128)(2,1)} %bitcast.16, bf16[8,40,256]{2,1,0:T(8,128)(2,1)} %bitcast.17, bf16[8,8,7168]{2,1,0:T(8,128)(2,1)} %up.1, bf16[8,8,7168]{2,1,0:T(8,128)(2,1)} %down.1), custom_call_target="tpu_custom_call" | custom-call | tf_op jit(solution)/shard_map/layer/pallas_call | solution.py:349
  264.7 0.0 copy-start.2
  264.7 2.2 convolution_convert_fusion.3
  266.9 2.1 convolution_convert_fusion.2
  269.0 0.0 copy-done.2
  269.0 0.0 copy-start.1
  269.0 0.9 copy.16
  269.9 0.6 copy-done.1
  270.5 0.9 copy.17
  (3 shorter events, 0.0 us)
Async XLA Ops:
  0.6 1.7 copy-start
  0.7 0.7 copy-start.4
  1.5 0.7 copy-start.5
  2.3 0.9 copy-start.3
  264.7 4.3 %copy-start.2 = (bf16[256,1792]{1,0:T(8,128)(2,1)S(1)}, bf16[256,1792]{1,0:T(8,128)(2,1)}, u32[]{:S(2)}) copy-start(bf16[256,1792]{1,0:T(8,128)(2,1)} %get-tuple-element.10) | copy-start | bytes 2752516
  269.0 1.5 copy-start.1

commit v3 on v2

v3 whole, which is shorter than its diff:
```python
import jax
import jax.numpy as jnp
from jax import lax
from jax.experimental import pallas as pl
from jax.experimental.pallas import tpu as pltpu
from jax.sharding import PartitionSpec as P

FF_W = 7168
E = 8
CAP = 34
SIDE = 4
HEAD = 32
TAIL = 8
MSG = HEAD + TAIL
BF = jnp.bfloat16
F32 = jnp.float32


def dot(a, b, ca, cb):
    return lax.dot_general(a, b, (((ca,), (cb,)), ((), ())), preferred_element_type=F32)


def mult(i, n):
    return pl.multiple_of(i, n)


def layer_kernel(
    x_msg, d_msg, up, down,
    y_out, dx_out, gu_out, gd_out,
    up_own, down_own, x_got, d_got, back_msg, sum_in, sum_far,
    xm, xt, dm, dt, tail32,
    pm, pt, ram, rat, rbm, rbt, sm, st, r2m, r2t, pre_m, pre_t, fm, ft,
    w_send, w_recv, t_send, t_recv, relay_send, relay_recv, fold_send, fold_recv, o_send, o_recv,
    rs_send, rs_recv, rs2_send, rs2_recv, ag_send, ag_recv, ag2_send, ag2_recv,
):
    n_dp = lax.axis_size("dp")
    quarters = n_dp // E
    blocks = n_dp // quarters
    hid = up_own.shape[2]
    own_f = xm.shape[1]
    j = lax.axis_index("dp")
    m = lax.axis_index("member")
    e, q = j // quarters, lax.rem(j, quarters)
    far_q = lax.rem(q + 2, 4)
    near_q = q + 1 - 2 * lax.rem(q, 2)
    near_far_q = lax.rem(near_q + 2, 4)
    cy, cx = m // SIDE, lax.rem(m, SIDE)
    half_rows = n_dp * HEAD // 2
    big = half_rows // SIDE
    small = big // SIDE
    t_rows = blocks * TAIL
    ht = t_rows // 2
    wide = pt.shape[2] // SIDE
    narrow = wide // SIDE
    started = []

    def first(h):
        return cx if h == 0 else cy

    def second(h):
        return cy if h == 0 else cx

    def peer_first(h, k):
        c = lax.rem(first(h) + k, SIDE)
        return c, {"member": cy * SIDE + c if h == 0 else c * SIDE + cx}

    def peer_second(h, k):
        c = lax.rem(second(h) + k, SIDE)
        return c, {"member": c * SIDE + cx if h == 0 else cy * SIDE + c}

    def shifted(i):
        step = i // 2 + 1
        return lax.rem(j + n_dp + step * (1 - 2 * lax.rem(i, 2)), n_dp)

    barrier = pltpu.get_barrier_semaphore()

    @pl.loop(0, n_dp - 1)
    def _(i):
        pl.semaphore_signal(barrier, inc=1, device_id={"dp": shifted(i)})

    for k in range(1, SIDE):
        pl.semaphore_signal(barrier, inc=1, device_id=peer_first(0, k)[1])
        pl.semaphore_signal(barrier, inc=1, device_id=peer_first(1, k)[1])
    pl.semaphore_wait(barrier, n_dp - 1 + 2 * (SIDE - 1))

    def remote(src, dst, send, recv, dev):
        return pltpu.make_async_remote_copy(
            src_ref=src, dst_ref=dst, send_sem=send, recv_sem=recv, device_id=dev
        )

    def start(copies):
        for c in copies:
            c.start()
        started.extend(copies)
        return copies

    def arrived(copies):
        for c in copies:
            c.wait_recv()

    def take(buf, sem):
        pltpu.make_async_copy(buf, buf, sem).wait()

    def weight_part(w, who):
        return w.at[who // quarters, :, pl.ds(mult(lax.rem(who, quarters) * hid, 128), hid)]

    def send_weights(n, w, own, lo, hi):
        @pl.loop(lo, hi)
        def _(i):
            who = shifted(i)
            remote(weight_part(w, who), own.at[j], w_send.at[n], w_recv.at[n], {"dp": who}).start()

    def send_tokens(n, msg, got):
        @pl.loop(1, blocks)
        def _(i):
            g = lax.rem(e + i, blocks)
            remote(msg.at[g], got.at[q, e], t_send.at[n], t_recv.at[n], {"dp": g * quarters + q}).start()

        pltpu.make_async_copy(msg.at[e], got.at[q, e], t_recv.at[n]).start()

    def relay_far(n, got):
        dev = {"dp": e * quarters + far_q}
        return start([remote(got.at[q], got.at[q], relay_send.at[n, 0], relay_recv.at[n, 0], dev)])

    def relay_near(n, got):
        dev = {"dp": e * quarters + near_q}
        return start(
            [
                remote(got.at[r], got.at[r], relay_send.at[n, 1 + i], relay_recv.at[n, 1 + i], dev)
                for i, r in enumerate((q, far_q))
            ]
        )

    def gather_rows(got, main, tail):
        @pl.loop(0, quarters)
        def _(r):
            for g in range(blocks):
                main[pl.ds(mult((r * blocks + g) * HEAD, HEAD), HEAD), :] = got[r, g, :HEAD, :]

        @pl.loop(0, blocks)
        def _(g):
            total = got[0, g, HEAD:, :].astype(F32)
            for r in range(1, quarters):
                total = total + got[r, g, HEAD:, :].astype(F32)
            tail32[pl.ds(mult(g * TAIL, TAIL), TAIL), :] = total

        tail[...] = tail32[...].astype(BF)

    def partial(t, main, tail, own):
        @pl.loop(0, hid // 256)
        def _(c):
            cols = pl.ds(mult(c * 256, 256), 256)
            w = own[:, :, cols].reshape(own_f, 256)
            pm[t, :, cols] = dot(main[...], w, 1, 0).astype(BF)
            pt[t, :, cols] = dot(tail[...], w, 1, 0).astype(BF)

    RIGHT, LEFT, FACING = 1, 3, 2
    hb, htb = big // 2, ht // 2

    def chunk_main(t, h, c, part):
        return pl.ds(mult(h * half_rows + c * big + part * hb, hb), hb)

    def chunk_tail(h, c, part):
        return pl.ds(h * ht + part * htb, htb), pl.ds(mult(c * wide, wide), wide)

    def rs_piece(t, h, to, c, part, dst_m, dst_t, n):
        dev = peer_first(h, to)[1]
        rows, cols = chunk_tail(h, c, part)
        return [
            remote(pm.at[t, chunk_main(t, h, c, part), :], dst_m, rs_send.at[t, h, n, 0], rs_recv.at[t, h, n, 0], dev),
            remote(pt.at[t, rows, cols], dst_t, rs_send.at[t, h, n, 1], rs_recv.at[t, h, n, 1], dev),
        ]

    def rs_pieces(t):
        passing, direct, joined = [], [], []
        for h in range(2):
            for side, to in enumerate((RIGHT, LEFT)):
                facing = peer_first(h, FACING)[0]
                c = peer_first(h, to)[0]
                passing.append(rs_piece(t, h, to, facing, side, ram.at[t, h, side], rat.at[t, h, side], side))
                direct.append(
                    rs_piece(t, h, to, c, 1 - side, rbm.at[t, h, side, 1 - side], rbt.at[t, h, side, 1 - side], 2 + side)
                )
                joined.append(
                    rs_piece(t, h, to, c, side, rbm.at[t, h, side, side], rbt.at[t, h, side, side], 4 + side)
                )
        return passing, direct, joined

    def rs_begin(t):
        passing, direct, joined = rs_pieces(t)
        for piece in passing + direct:
            start(piece)
        return passing, direct, joined

    def rs_join(t, pieces):
        passing, direct, joined = pieces
        n = 0
        for h in range(2):
            for side, to in enumerate((RIGHT, LEFT)):
                arrived(passing[n])
                c = peer_first(h, to)[0]
                base = h * half_rows + c * big + side * hb

                @pl.loop(0, hb // 16)
                def _(i):
                    rows = pl.ds(mult(base + i * 16, 16), 16)
                    got = ram[t, h, side, pl.ds(mult(i * 16, 16), 16), :]
                    pm[t, rows, :] = (pm[t, rows, :].astype(F32) + got.astype(F32)).astype(BF)

                rows, cols = chunk_tail(h, c, side)
                pt[t, rows, cols] = (pt[t, rows, cols].astype(F32) + rat[t, h, side].astype(F32)).astype(BF)
                start(joined[n])
                n += 1
        for piece in direct + joined:
            arrived(piece)

    def sum_first(t):
        for h in range(2):
            for part in range(2):
                base = h * half_rows + first(h) * big + part * hb

                @pl.loop(0, hb // 16)
                def _(i):
                    rows = pl.ds(mult(i * 16, 16), 16)
                    total = pm[t, pl.ds(mult(base + i * 16, 16), 16), :].astype(F32)
                    for side in range(2):
                        total = total + rbm[t, h, side, part, rows, :].astype(F32)
                    sm[t, h, pl.ds(mult(part * hb + i * 16, 16), 16), :] = total.astype(BF)

                rows, cols = chunk_tail(h, first(h), part)
                total = pt[t, rows, cols].astype(F32)
                for side in range(2):
                    total = total + rbt[t, h, side, part].astype(F32)
                st[t, h, part * htb : (part + 1) * htb, :] = total.astype(BF)

    def rs_small(t):
        out = []
        for h in range(2):
            for k in range(1, SIDE):
                c, dev = peer_second(h, k)
                sems = lambda n: (rs2_send.at[t, h, k - 1, n], rs2_recv.at[t, h, k - 1, n])
                out += [
                    remote(sm.at[t, h, pl.ds(mult(c * small, small), small), :], r2m.at[t, h, k - 1], *sems(0), dev),
                    remote(st.at[t, h, :, pl.ds(mult(c * narrow, narrow), narrow)], r2t.at[t, h, k - 1], *sems(1), dev),
                ]
        return start(out)

    def owned_rows(h):
        return pl.ds(mult(h * half_rows + first(h) * big + second(h) * small, small), small)

    def owned_cols(h):
        return pl.ds(mult(first(h) * wide + second(h) * narrow, narrow), narrow)

    def finish(t, fn):
        for h in range(2):

            @pl.loop(0, small // 16)
            def _(i):
                rows = pl.ds(mult(i * 16, 16), 16)
                total = sm[t, h, pl.ds(mult(second(h) * small + i * 16, 16), 16), :].astype(F32)
                for k in range(SIDE - 1):
                    total = total + r2m[t, h, k, rows, :].astype(F32)
                start_row = h * half_rows + first(h) * big + second(h) * small
                fm[t, pl.ds(mult(start_row + i * 16, 16), 16), :] = fn(total, pre_m.at[h, rows, :]).astype(BF)

            total = st[t, h, :, pl.ds(mult(second(h) * narrow, narrow), narrow)].astype(F32)
            for k in range(SIDE - 1):
                total = total + r2t[t, h, k].astype(F32)
            ft[t, pl.ds(h * ht, ht), owned_cols(h)] = fn(total, pre_t.at[h]).astype(BF)

    def silu(total, keep):
        keep[...] = total
        return total / (1.0 + jnp.exp(-total))

    def silu_back(total, keep):
        pre = keep[...]
        s = 1.0 / (1.0 + jnp.exp(-pre))
        return total * s * (1.0 + pre * (1.0 - s))

    def ag_small(t):
        out = []
        for h in range(2):
            for k in range(1, SIDE):
                dev = peer_second(h, k)[1]
                for n, ref in enumerate(
                    (fm.at[t, owned_rows(h), :], ft.at[t, pl.ds(h * ht, ht), owned_cols(h)])
                ):
                    out.append(remote(ref, ref, ag_send.at[t, h, k - 1, n], ag_recv.at[t, h, k - 1, n], dev))
        return start(out)

    def ag_piece(t, h, to, c, part, n):
        dev = peer_first(h, to)[1]
        rows, cols = chunk_tail(h, c, part)
        return [
            remote(ref, ref, ag2_send.at[t, h, n, i], ag2_recv.at[t, h, n, i], dev)
            for i, ref in enumerate((fm.at[t, chunk_main(t, h, c, part), :], ft.at[t, rows, cols]))
        ]

    def ag_big(t):
        early, late, passed = [], [], []
        for h in range(2):
            for side, to in enumerate((RIGHT, LEFT)):
                early.append(start(ag_piece(t, h, to, first(h), side, side)))
        for h in range(2):
            for side, to in enumerate((RIGHT, LEFT)):
                late.append(start(ag_piece(t, h, to, first(h), 1 - side, 2 + side)))
        n = 0
        for h in range(2):
            for side, to in enumerate((RIGHT, LEFT)):
                arrived(early[n])
                back_c = peer_first(h, LEFT if to == RIGHT else RIGHT)[0]
                passed.append(start(ag_piece(t, h, to, back_c, side, 4 + side)))
                n += 1
        return late + passed

    def settle(pieces):
        for piece in pieces:
            arrived(piece)

    def back(t, own):
        flat = own[...].reshape(own_f, hid)
        rows = blocks * HEAD

        @pl.loop(0, quarters)
        def _(r):
            part = dot(fm[t, pl.ds(mult(r * rows, rows), rows), :], flat, 1, 1).astype(BF)
            for g in range(blocks):
                back_msg[t, r, g, :HEAD, :] = part[g * HEAD : (g + 1) * HEAD, :]

        tail32[...] = dot(ft[t, :, :hid], flat, 1, 1)

        @pl.loop(0, blocks)
        def _(g):
            for r in range(quarters):
                back_msg[t, r, g, HEAD:, :] = tail32[pl.ds(mult(g * TAIL, TAIL), TAIL), :].astype(BF)

    def fold_near(t):
        dev = {"dp": e * quarters + near_q}
        return start(
            [
                remote(back_msg.at[t, r], sum_in.at[t, i], fold_send.at[t, i], fold_recv.at[t, i], dev)
                for i, r in enumerate((near_q, near_far_q))
            ]
        )

    def fold_far(t):
        for i, r in ((1, far_q), (0, q)):
            for g in range(blocks):
                total = back_msg[t, r, g].astype(F32) + sum_in[t, i, g].astype(F32)
                back_msg[t, r, g] = total.astype(BF)
            if i == 1:
                dev = {"dp": e * quarters + far_q}
                out = start(
                    [remote(back_msg.at[t, r], sum_far.at[t], fold_send.at[t, 2], fold_recv.at[t, 2], dev)]
                )
        return out

    def give_back(t, got):
        for g in range(blocks):
            total = back_msg[t, q, g].astype(F32) + sum_far[t, g].astype(F32)
            back_msg[t, q, g] = total.astype(BF)

        @pl.loop(1, blocks)
        def _(i):
            g = lax.rem(e + i, blocks)
            remote(back_msg.at[t, q, g], got.at[e], o_send.at[t], o_recv.at[t], {"dp": g * quarters + q}).start()

        pltpu.make_async_copy(back_msg.at[t, q, e], got.at[e], o_recv.at[t]).start()

    def gradient(main, tail, t, out):
        left_m, left_t = main[...], tail[...]

        @pl.loop(0, hid // 256)
        def _(c):
            cols = pl.ds(mult(c * 256, 256), 256)
            g = dot(left_m, fm[t, :, cols], 0, 0) + dot(left_t, ft[t, :, cols], 0, 0)
            out[:, cols] = g.astype(BF)

    send_tokens(0, x_msg, x_got)
    send_tokens(1, d_msg, d_got)
    send_weights(0, up, up_own, 0, 8)
    pltpu.make_async_copy(weight_part(up, j), up_own.at[j], w_recv.at[0]).start()
    pltpu.make_async_copy(weight_part(down, j), down_own.at[j], w_recv.at[1]).start()
    take(x_got.at[q], t_recv.at[0])
    xf = relay_far(0, x_got)
    take(d_got.at[q], t_recv.at[1])
    df = relay_far(1, d_got)
    send_weights(0, up, up_own, 8, n_dp - 1)
    arrived(xf)
    xn = relay_near(0, x_got)
    arrived(df)
    dn = relay_near(1, d_got)
    send_weights(1, down, down_own, 0, n_dp - 1)
    pt[:, :, hid:] = jnp.zeros((2, t_rows, pt.shape[2] - hid), BF)
    arrived(xn)
    gather_rows(x_got, xm, xt)
    arrived(dn)
    gather_rows(d_got, dm, dt)

    take(up_own, w_recv.at[0])
    partial(0, xm, xt, up_own)
    rs_join(0, rs_begin(0))
    sum_first(0)
    arrived(rs_small(0))
    finish(0, silu)
    arrived(ag_small(0))
    ag0 = ag_big(0)

    take(down_own, w_recv.at[1])
    partial(1, dm, dt, down_own)
    rs1 = rs_begin(1)
    settle(ag0)
    rs_join(1, rs1)
    sum_first(1)
    small1 = rs_small(1)
    back(0, down_own)
    near0 = fold_near(0)
    arrived(small1)
    finish(1, silu_back)
    gather1 = ag_small(1)
    arrived(near0)
    far0 = fold_far(0)
    arrived(gather1)
    ag1 = ag_big(1)
    arrived(far0)
    give_back(0, y_out)
    gradient(dm, dt, 0, gd_out)
    settle(ag1)
    back(1, up_own)
    near1 = fold_near(1)
    arrived(near1)
    far1 = fold_far(1)
    arrived(far1)
    give_back(1, dx_out)
    gradient(xm, xt, 1, gu_out)
    take(y_out, o_recv.at[0])
    take(dx_out, o_recv.at[1])
    for c in started:
        c.wait_send()
    for n, own in enumerate((up_own, down_own)):
        take(own.at[pl.ds(0, n_dp - 1)], w_send.at[n])
    for n, got in enumerate((x_got, d_got)):
        take(got.at[0, pl.ds(0, blocks - 1)], t_send.at[n])
    for n, got in enumerate((y_out, dx_out)):
        take(got.at[pl.ds(0, blocks - 1)], o_send.at[n])


def layer(x_msg, d_msg, up, down):
    n_dp = lax.axis_size("dp")
    own_f = x_msg.shape[2]
    rows = up.shape[1]
    quarters = n_dp // E
    blocks = n_dp // quarters
    hid = up.shape[2] // quarters
    main = n_dp * HEAD
    tails = blocks * TAIL
    wide = -(-hid // (SIDE * SIDE * 128)) * SIDE * SIDE * 128
    big = main // 2 // SIDE
    small = big // SIDE
    ht = tails // 2
    vm = pltpu.VMEM
    dma = pltpu.SemaphoreType.DMA
    return pl.pallas_call(
        layer_kernel,
        name="layer",
        out_shape=(
            jax.ShapeDtypeStruct((E, MSG, own_f), BF),
            jax.ShapeDtypeStruct((E, MSG, own_f), BF),
            jax.ShapeDtypeStruct((own_f, hid), BF),
            jax.ShapeDtypeStruct((own_f, hid), BF),
        ),
        in_specs=[pl.BlockSpec(memory_space=pltpu.VMEM)] * 2 + [pl.BlockSpec(memory_space=pl.ANY)] * 2,
        out_specs=[pl.BlockSpec(memory_space=pltpu.VMEM)] * 4,
        scratch_shapes=[
            vm((n_dp, rows, hid), BF), vm((n_dp, rows, hid), BF),
            vm((quarters, blocks, MSG, own_f), BF), vm((quarters, blocks, MSG, own_f), BF),
            vm((2, quarters, blocks, MSG, own_f), BF), vm((2, 2, blocks, MSG, own_f), BF),
            vm((2, blocks, MSG, own_f), BF),
            vm((main, own_f), BF), vm((tails, own_f), BF),
            vm((main, own_f), BF), vm((tails, own_f), BF),
            vm((tails, own_f), F32),
            vm((2, main, hid), BF), vm((2, tails, wide), BF),
            vm((2, 2, 2, big // 2, hid), BF), vm((2, 2, 2, ht // 2, wide // SIDE), BF),
            vm((2, 2, 2, 2, big // 2, hid), BF), vm((2, 2, 2, 2, ht // 2, wide // SIDE), BF),
            vm((2, 2, big, hid), BF), vm((2, 2, ht, wide // SIDE), BF),
            vm((2, 2, SIDE - 1, small, hid), BF), vm((2, 2, SIDE - 1, ht, wide // SIDE // SIDE), BF),
            vm((2, small, hid), F32), vm((2, ht, wide // SIDE // SIDE), F32),
            vm((2, main, hid), BF), vm((2, tails, wide), BF),
            dma((2,)), dma((2,)), dma((2,)), dma((2,)), dma((2, 3)), dma((2, 3)), dma((2, 3)), dma((2, 3)),
            dma((2,)), dma((2,)),
            dma((2, 2, 6, 2)), dma((2, 2, 6, 2)), dma((2, 2, SIDE - 1, 2)), dma((2, 2, SIDE - 1, 2)),
            dma((2, 2, SIDE - 1, 2)), dma((2, 2, SIDE - 1, 2)), dma((2, 2, 6, 2)), dma((2, 2, 6, 2)),
        ],
        compiler_params=pltpu.CompilerParams(
            collective_id=0, has_side_effects=True, vmem_limit_bytes=58 * 2**20
        ),
    )(x_msg, d_msg, up, down)


def body(tokens, routes, route_weights, up_stacked, down_stacked, cotangent):
    experts = jnp.arange(E, dtype=jnp.int32)
    named = routes[:, :, None] == experts[None, None, :]
    chosen = jnp.sum(named.astype(F32), axis=1)
    rows = jnp.arange(routes.shape[0], dtype=jnp.int32)
    earlier = (rows[None, :] < rows[:, None]).astype(BF)
    before = jnp.dot(earlier, chosen.astype(BF), preferred_element_type=F32).astype(jnp.int32)
    slot_pos = jnp.sum(jnp.where(named, before[:, None, :], 0), axis=2)
    shift = 2 * lax.rem(lax.axis_index("dp"), 4)
    target = routes * MSG + slot_pos + jnp.where(slot_pos >= HEAD, shift, 0)
    slot_hits = jnp.arange(E * MSG, dtype=jnp.int32)[:, None, None] == target[None, :, :]
    pick_table = jnp.sum(slot_hits.astype(F32), axis=2)
    weighted = jnp.sum(jnp.where(slot_hits, route_weights[None, :, :], 0.0), axis=2)
    features = tokens.shape[1]
    x_msg = jnp.dot(pick_table.astype(BF), tokens, preferred_element_type=F32).astype(BF)
    d_msg = jnp.dot(weighted, cotangent.astype(F32), precision=lax.Precision.HIGHEST).astype(BF)
    y_slots, dx_slots, g_up, g_down = layer(
        x_msg.reshape(E, MSG, features), d_msg.reshape(E, MSG, features), up_stacked, down_stacked
    )
    y_slots = y_slots.reshape(E * MSG, features).astype(F32)
    dx_slots = dx_slots.reshape(E * MSG, features).astype(F32)
    mixed = jnp.dot(weighted.T, y_slots, precision=lax.Precision.HIGHEST).astype(BF)
    grad_tokens = jnp.dot(pick_table.T, dx_slots, precision=lax.Precision.HIGHEST).astype(BF)
    return (mixed, grad_tokens, g_up[None], g_down[None])


def solution(mesh):
    placed = (
        P("dp", "member"),
        P("dp", None),
        P("dp", None),
        P(None, ("member", "dp"), None),
        P(None, ("member", "dp"), None),
        P("dp", "member"),
    )
    return jax.shard_map(
        body,
        mesh=mesh,
        in_specs=placed,
        out_specs=(
            P("dp", "member"),
            P("dp", "member"),
            P("dp", "member", None),
            P("dp", "member", None),
        ),
        check_vma=False,
    )
```

time: 272 us -> 232 us (0.85)
  the two profiles are of different devices: /device:TPU:32 before, /device:TPU:1 now
where the time goes in v3:
time: 232 us
  Pallas kernels  222 us (96%)
  matrix products  4.87 us (2%)
  local copies, waits for them, and re-layouts  4.55 us (2%)
    pallas_call x1, Pallas kernels, layer(): pl.pallas_call(layer_kernel, name='layer', out_shape=(jax.ShapeDtypeStruc...  222 us

profile of v3, /device:TPU:1, one launch (start us, length us, event | category | flops | bytes accessed | tf_op | source)
XLA Modules:
  0.0 232.2 jit_solution(9817662812457030217)
XLA Ops:
  0.6 0.0 copy-start
  0.7 0.0 copy-start.4
  0.7 0.7 copy-done.4
  1.4 0.1 convolution_convert_fusion.4
  1.5 0.0 copy-start.5
  1.6 0.7 copy-done.5
  2.2 0.1 convert_reduce_fusion
  2.3 0.0 copy-done
  2.3 0.0 copy-start.3
  2.3 0.9 convolution_convert_fusion.1
  3.2 0.0 copy-done.3
  3.2 0.9 convolution_convert_fusion
  4.1 222.0 %layer.1 = (bf16[8,40,256]{2,1,0:T(8,128)(2,1)}, bf16[8,40,256]{2,1,0:T(8,128)(2,1)}, bf16[256,1792]{1,0:T(8,128)(2,1)}, bf16[256,1792]{1,0:T(8,128)(2,1)}) custom-call(bf16[8,40,256]{2,1,0:T(8,128)(2,1)} %bitcast.16, bf16[8,40,256]{2,1,0:T(8,128)(2,1)} %bitcast.17, bf16[8,8,7168]{2,1,0:T(8,128)(2,1)} %up.1, bf16[8,8,7168]{2,1,0:T(8,128)(2,1)} %down.1), custom_call_target="tpu_custom_call" | custom-call | tf_op jit(solution)/shard_map/layer/pallas_call | solution.py:463
  226.1 0.0 copy-start.2
  226.1 1.9 convolution_convert_fusion.3
  228.1 0.0 copy-done.2
  228.1 1.0 convolution_convert_fusion.2
  229.1 0.0 copy-start.1
  229.1 2.2 copy.16
  231.3 0.0 copy-done.1
  231.3 0.9 copy.17
  (3 shorter events, 0.0 us)
Async XLA Ops:
  0.6 1.7 copy-start
  0.7 0.7 copy-start.4
  1.5 0.7 copy-start.5
  2.3 0.9 copy-start.3
  226.1 2.0 copy-start.2
  229.1 2.2 copy-start.1

commit v4 on v3

v4 whole, which is shorter than its diff:
```python
import jax
import jax.numpy as jnp
from jax import lax
from jax.experimental import pallas as pl
from jax.experimental.pallas import tpu as pltpu
from jax.sharding import PartitionSpec as P

FF_W = 7168
E = 8
CAP = 34
SIDE = 4
PARTS = 2
HEAD = 32
TAIL = 8
MSG = HEAD + TAIL
BF = jnp.bfloat16
F32 = jnp.float32


def dot(a, b, ca, cb):
    return lax.dot_general(a, b, (((ca,), (cb,)), ((), ())), preferred_element_type=F32)


def mult(i, n):
    return pl.multiple_of(i, n)


def layer_kernel(
    x_msg, d_msg, up, down,
    y_out, dx_out, gu_out, gd_out,
    up_own, down_own, x_got, d_got, back_msg, sum_in, sum_far,
    xm, xt, dm, dt, tail32, early,
    pm, pt, ram, rat, rbm, rbt, sm, st, r2m, r2t, pre_m, pre_t, fm, ft,
    w_send, w_recv, t_send, t_recv, relay_send, relay_recv, fold_send, fold_recv, o_send, o_recv,
    rs_send, rs_recv, rs2_send, rs2_recv, ag_send, ag_recv, ag2_send, ag2_recv,
):
    n_dp = lax.axis_size("dp")
    quarters = n_dp // E
    blocks = n_dp // quarters
    hw = up_own.shape[3]
    hid = PARTS * hw
    last = PARTS - 1
    own_f = xm.shape[1]
    j = lax.axis_index("dp")
    m = lax.axis_index("member")
    e, q = j // quarters, lax.rem(j, quarters)
    far_q = lax.rem(q + 2, 4)
    near_q = q + 1 - 2 * lax.rem(q, 2)
    near_far_q = lax.rem(near_q + 2, 4)
    cy, cx = m // SIDE, lax.rem(m, SIDE)
    half_rows = n_dp * HEAD // 2
    big = half_rows // SIDE
    small = big // SIDE
    t_rows = blocks * TAIL
    ht = t_rows // 2
    wide = pt.shape[2] // SIDE
    narrow = wide // SIDE
    started = []

    def first(h):
        return cx if h == 0 else cy

    def second(h):
        return cy if h == 0 else cx

    def peer_first(h, k):
        c = lax.rem(first(h) + k, SIDE)
        return c, {"member": cy * SIDE + c if h == 0 else c * SIDE + cx}

    def peer_second(h, k):
        c = lax.rem(second(h) + k, SIDE)
        return c, {"member": c * SIDE + cx if h == 0 else cy * SIDE + c}

    def shifted(i):
        step = i // 2 + 1
        return lax.rem(j + n_dp + step * (1 - 2 * lax.rem(i, 2)), n_dp)

    barrier = pltpu.get_barrier_semaphore()

    @pl.loop(0, n_dp - 1)
    def _(i):
        pl.semaphore_signal(barrier, inc=1, device_id={"dp": shifted(i)})

    for k in range(1, SIDE):
        pl.semaphore_signal(barrier, inc=1, device_id=peer_first(0, k)[1])
        pl.semaphore_signal(barrier, inc=1, device_id=peer_first(1, k)[1])
    pl.semaphore_wait(barrier, n_dp - 1 + 2 * (SIDE - 1))

    def remote(src, dst, send, recv, dev):
        return pltpu.make_async_remote_copy(
            src_ref=src, dst_ref=dst, send_sem=send, recv_sem=recv, device_id=dev
        )

    def start(copies):
        for c in copies:
            c.start()
        started.extend(copies)
        return copies

    def arrived(copies):
        for c in copies:
            c.wait_recv()

    def take(buf, sem):
        pltpu.make_async_copy(buf, buf, sem).wait()

    def weight_part(w, u, who):
        column = lax.rem(who, quarters) * hid + u * hw
        return w.at[who // quarters, :, pl.ds(mult(column, 128), hw)]

    def send_weights(t, u, w, own, lo, hi):
        n = t * PARTS + u

        @pl.loop(lo, hi)
        def _(i):
            who = shifted(i)
            remote(weight_part(w, u, who), own.at[u, j], w_send.at[n], w_recv.at[n], {"dp": who}).start()

    def keep_weights(t, w, own):
        for u in range(PARTS):
            pltpu.make_async_copy(weight_part(w, u, j), own.at[u, j], w_recv.at[t * PARTS + u]).start()

    def send_tokens(n, msg, got):
        @pl.loop(1, blocks)
        def _(i):
            g = lax.rem(e + i, blocks)
            remote(msg.at[g], got.at[q, e], t_send.at[n], t_recv.at[n], {"dp": g * quarters + q}).start()

        pltpu.make_async_copy(msg.at[e], got.at[q, e], t_recv.at[n]).start()

    def relay_far(n, got):
        dev = {"dp": e * quarters + far_q}
        return start([remote(got.at[q], got.at[q], relay_send.at[n, 0], relay_recv.at[n, 0], dev)])

    def relay_near(n, got):
        dev = {"dp": e * quarters + near_q}
        return start(
            [
                remote(got.at[r], got.at[r], relay_send.at[n, 1 + i], relay_recv.at[n, 1 + i], dev)
                for i, r in enumerate((q, far_q))
            ]
        )

    def gather_rows(got, main, tail):
        @pl.loop(0, quarters)
        def _(r):
            for g in range(blocks):
                main[pl.ds(mult((r * blocks + g) * HEAD, HEAD), HEAD), :] = got[r, g, :HEAD, :]

        @pl.loop(0, blocks)
        def _(g):
            total = got[0, g, HEAD:, :].astype(F32)
            for r in range(1, quarters):
                total = total + got[r, g, HEAD:, :].astype(F32)
            tail32[pl.ds(mult(g * TAIL, TAIL), TAIL), :] = total

        tail[...] = tail32[...].astype(BF)

    def flat(own, u):
        return own[u].reshape(own_f, hw)

    def partial(t, u, main, tail, own):
        rows = n_dp * HEAD // 4

        @pl.loop(0, 4)
        def _(i):
            block = pl.ds(mult(i * rows, rows), rows)
            pm[t, u, block, :] = dot(main[block, :], flat(own, u), 1, 0).astype(BF)

        if u == last:
            for v in range(PARTS):
                pt[t, :, v * hw : (v + 1) * hw] = dot(tail[...], flat(own, v), 1, 0).astype(BF)

    RIGHT, LEFT, FACING = 1, 3, 2
    hb, htb = big // 2, ht // 2

    def chunk_main(h, c, part):
        return pl.ds(mult(h * half_rows + c * big + part * hb, hb), hb)

    def chunk_tail(h, c, part):
        return pl.ds(h * ht + part * htb, htb), pl.ds(mult(c * wide, wide), wide)

    def rs_piece(t, u, h, to, c, part, dst_m, dst_t, n):
        dev = peer_first(h, to)[1]
        p = t * PARTS + u
        src = pm.at[t, u, chunk_main(h, c, part), :]
        out = [remote(src, dst_m, rs_send.at[p, h, n, 0], rs_recv.at[p, h, n, 0], dev)]
        if u == last:
            rows, cols = chunk_tail(h, c, part)
            out.append(remote(pt.at[t, rows, cols], dst_t, rs_send.at[p, h, n, 1], rs_recv.at[p, h, n, 1], dev))
        return out

    def rs_begin(t, u):
        passing, direct, joined = [], [], []
        for h in range(2):
            for side, to in enumerate((RIGHT, LEFT)):
                facing = peer_first(h, FACING)[0]
                c = peer_first(h, to)[0]
                a, b = (ram.at[t, u, h, side], rat.at[t, h, side]), (rbm.at[t, u, h, side], rbt.at[t, h, side])
                passing.append(rs_piece(t, u, h, to, facing, side, *a, side))
                direct.append(rs_piece(t, u, h, to, c, 1 - side, b[0].at[1 - side], b[1].at[1 - side], 2 + side))
                joined.append(rs_piece(t, u, h, to, c, side, b[0].at[side], b[1].at[side], 4 + side))
        for piece in passing + direct:
            start(piece)
        return passing, direct, joined

    def rs_join(t, u, pieces):
        passing, direct, joined = pieces
        n = 0
        for h in range(2):
            for side, to in enumerate((RIGHT, LEFT)):
                arrived(passing[n])
                c = peer_first(h, to)[0]
                base = h * half_rows + c * big + side * hb

                @pl.loop(0, hb // 16)
                def _(i):
                    rows = pl.ds(mult(base + i * 16, 16), 16)
                    got = ram[t, u, h, side, pl.ds(mult(i * 16, 16), 16), :]
                    pm[t, u, rows, :] = (pm[t, u, rows, :].astype(F32) + got.astype(F32)).astype(BF)

                if u == last:
                    rows, cols = chunk_tail(h, c, side)
                    pt[t, rows, cols] = (pt[t, rows, cols].astype(F32) + rat[t, h, side].astype(F32)).astype(BF)
                start(joined[n])
                n += 1
        for piece in direct + joined:
            arrived(piece)

    def sum_first(t, u):
        for h in range(2):
            for part in range(2):
                base = h * half_rows + first(h) * big + part * hb

                @pl.loop(0, hb // 16)
                def _(i):
                    rows = pl.ds(mult(i * 16, 16), 16)
                    total = pm[t, u, pl.ds(mult(base + i * 16, 16), 16), :].astype(F32)
                    for side in range(2):
                        total = total + rbm[t, u, h, side, part, rows, :].astype(F32)
                    sm[t, u, h, pl.ds(mult(part * hb + i * 16, 16), 16), :] = total.astype(BF)

                if u == last:
                    rows, cols = chunk_tail(h, first(h), part)
                    total = pt[t, rows, cols].astype(F32)
                    for side in range(2):
                        total = total + rbt[t, h, side, part].astype(F32)
                    st[t, h, part * htb : (part + 1) * htb, :] = total.astype(BF)

    def rs_small(t, u):
        out = []
        p = t * PARTS + u
        for h in range(2):
            for k in range(1, SIDE):
                c, dev = peer_second(h, k)
                pairs = [(sm.at[t, u, h, pl.ds(mult(c * small, small), small), :], r2m.at[t, u, h, k - 1])]
                if u == last:
                    pairs.append((st.at[t, h, :, pl.ds(mult(c * narrow, narrow), narrow)], r2t.at[t, h, k - 1]))
                for n, (src, dst) in enumerate(pairs):
                    out.append(remote(src, dst, rs2_send.at[p, h, k - 1, n], rs2_recv.at[p, h, k - 1, n], dev))
        return start(out)

    def owned_rows(h):
        return pl.ds(mult(h * half_rows + first(h) * big + second(h) * small, small), small)

    def owned_cols(h):
        return pl.ds(mult(first(h) * wide + second(h) * narrow, narrow), narrow)

    def finish(t, u, fn):
        for h in range(2):

            @pl.loop(0, small // 16)
            def _(i):
                rows = pl.ds(mult(i * 16, 16), 16)
                total = sm[t, u, h, pl.ds(mult(second(h) * small + i * 16, 16), 16), :].astype(F32)
                for k in range(SIDE - 1):
                    total = total + r2m[t, u, h, k, rows, :].astype(F32)
                start_row = h * half_rows + first(h) * big + second(h) * small
                fm[t, u, pl.ds(mult(start_row + i * 16, 16), 16), :] = fn(total, pre_m.at[u, h, rows, :]).astype(BF)

            if u == last:
                total = st[t, h, :, pl.ds(mult(second(h) * narrow, narrow), narrow)].astype(F32)
                for k in range(SIDE - 1):
                    total = total + r2t[t, h, k].astype(F32)
                ft[t, pl.ds(h * ht, ht), owned_cols(h)] = fn(total, pre_t.at[h]).astype(BF)

    def silu(total, keep):
        keep[...] = total
        return total / (1.0 + jnp.exp(-total))

    def silu_back(total, keep):
        pre = keep[...]
        s = 1.0 / (1.0 + jnp.exp(-pre))
        return total * s * (1.0 + pre * (1.0 - s))

    def ag_small(t, u):
        out = []
        p = t * PARTS + u
        for h in range(2):
            for k in range(1, SIDE):
                dev = peer_second(h, k)[1]
                refs = [fm.at[t, u, owned_rows(h), :]]
                if u == last:
                    refs.append(ft.at[t, pl.ds(h * ht, ht), owned_cols(h)])
                for n, ref in enumerate(refs):
                    out.append(remote(ref, ref, ag_send.at[p, h, k - 1, n], ag_recv.at[p, h, k - 1, n], dev))
        return start(out)

    def ag_piece(t, u, h, to, c, part, n):
        dev = peer_first(h, to)[1]
        p = t * PARTS + u
        refs = [fm.at[t, u, chunk_main(h, c, part), :]]
        if u == last:
            rows, cols = chunk_tail(h, c, part)
            refs.append(ft.at[t, rows, cols])
        return [
            remote(ref, ref, ag2_send.at[p, h, n, i], ag2_recv.at[p, h, n, i], dev) for i, ref in enumerate(refs)
        ]

    def ag_big(t, u):
        soon, late = [], []
        for h in range(2):
            for side, to in enumerate((RIGHT, LEFT)):
                soon.append(start(ag_piece(t, u, h, to, first(h), side, side)))
        for h in range(2):
            for side, to in enumerate((RIGHT, LEFT)):
                late.append(start(ag_piece(t, u, h, to, first(h), 1 - side, 2 + side)))
        return soon, late

    def ag_pass(t, u, pieces):
        soon, late = pieces
        passed = []
        n = 0
        for h in range(2):
            for side, to in enumerate((RIGHT, LEFT)):
                arrived(soon[n])
                back_c = peer_first(h, LEFT if to == RIGHT else RIGHT)[0]
                passed.append(start(ag_piece(t, u, h, to, back_c, side, 4 + side)))
                n += 1
        return late + passed

    def settle(pieces):
        for piece in pieces:
            arrived(piece)

    share = blocks * HEAD

    def share_rows(r):
        return pl.ds(mult(r * share, share), share)

    def back_early(t, own):
        @pl.loop(0, quarters)
        def _(r):
            total = dot(fm[t, 0, share_rows(r), :], flat(own, 0), 1, 1)
            for u in range(1, last):
                total = total + dot(fm[t, u, share_rows(r), :], flat(own, u), 1, 1)
            early[share_rows(r), :] = total

    def back_tail(t, own):
        total = dot(ft[t, :, :hw], flat(own, 0), 1, 1)
        for u in range(1, PARTS):
            total = total + dot(ft[t, :, u * hw : (u + 1) * hw], flat(own, u), 1, 1)
        tail32[...] = total

    def back_share(t, own, r):
        total = early[share_rows(r), :] + dot(fm[t, last, share_rows(r), :], flat(own, last), 1, 1)
        part = total.astype(BF)
        for g in range(blocks):
            back_msg[t, r, g, :HEAD, :] = part[g * HEAD : (g + 1) * HEAD, :]
            back_msg[t, r, g, HEAD:, :] = tail32[g * TAIL : (g + 1) * TAIL, :].astype(BF)

    def fold_near(t, own):
        dev = {"dp": e * quarters + near_q}
        out = []
        for i, r in ((1, near_far_q), (0, near_q)):
            back_share(t, own, r)
            out += start([remote(back_msg.at[t, r], sum_in.at[t, i], fold_send.at[t, i], fold_recv.at[t, i], dev)])
        for r in (far_q, q):
            back_share(t, own, r)
        return out

    def fold_far(t, near):
        for n, (i, r) in enumerate(((1, far_q), (0, q))):
            arrived(near[n : n + 1])
            for g in range(blocks):
                total = back_msg[t, r, g].astype(F32) + sum_in[t, i, g].astype(F32)
                back_msg[t, r, g] = total.astype(BF)
            if i == 1:
                dev = {"dp": e * quarters + far_q}
                out = start(
                    [remote(back_msg.at[t, r], sum_far.at[t], fold_send.at[t, 2], fold_recv.at[t, 2], dev)]
                )
        return out

    def give_back(t, got):
        for g in range(blocks):
            total = back_msg[t, q, g].astype(F32) + sum_far[t, g].astype(F32)
            back_msg[t, q, g] = total.astype(BF)

        @pl.loop(1, blocks)
        def _(i):
            g = lax.rem(e + i, blocks)
            remote(back_msg.at[t, q, g], got.at[e], o_send.at[t], o_recv.at[t], {"dp": g * quarters + q}).start()

        pltpu.make_async_copy(back_msg.at[t, q, e], got.at[e], o_recv.at[t]).start()

    def gradient(main, tail, t, u, out):
        @pl.loop(0, hw // 128)
        def _(c):
            at = mult(c * 128, 128)
            g = dot(main[...], fm[t, u, :, pl.ds(at, 128)], 0, 0)
            g = g + dot(tail[...], ft[t, :, pl.ds(u * hw + at, 128)], 0, 0)
            out[:, pl.ds(u * hw + at, 128)] = g.astype(BF)

    send_tokens(0, x_msg, x_got)
    send_weights(0, 0, up, up_own, 0, 8)
    keep_weights(0, up, up_own)
    keep_weights(1, down, down_own)
    take(x_got.at[q], t_recv.at[0])
    xf = relay_far(0, x_got)
    send_weights(0, 0, up, up_own, 8, n_dp - 1)
    arrived(xf)
    xn = relay_near(0, x_got)
    send_weights(0, 1, up, up_own, 0, n_dp - 1)
    pt[:, :, hid:] = jnp.zeros((2, t_rows, pt.shape[2] - hid), BF)
    arrived(xn)
    gather_rows(x_got, xm, xt)

    take(up_own.at[0], w_recv.at[0])
    partial(0, 0, xm, xt, up_own)
    rs_0 = rs_begin(0, 0)
    send_tokens(1, d_msg, d_got)
    send_weights(1, 0, down, down_own, 0, n_dp - 1)
    rs_join(0, 0, rs_0)
    sum_first(0, 0)
    small_0 = rs_small(0, 0)

    take(up_own.at[1], w_recv.at[1])
    partial(0, 1, xm, xt, up_own)
    rs_1 = rs_begin(0, 1)
    take(d_got.at[q], t_recv.at[1])
    df = relay_far(1, d_got)
    arrived(small_0)
    finish(0, 0, silu)
    gather_0 = ag_small(0, 0)
    send_weights(1, 1, down, down_own, 0, n_dp - 1)
    rs_join(0, 1, rs_1)
    sum_first(0, 1)
    small_1 = rs_small(0, 1)
    arrived(gather_0)
    ag_0 = ag_big(0, 0)
    arrived(df)
    dn = relay_near(1, d_got)
    arrived(dn)
    gather_rows(d_got, dm, dt)

    take(down_own.at[0], w_recv.at[2])
    partial(1, 0, dm, dt, down_own)
    rs_2 = rs_begin(1, 0)
    arrived(small_1)
    finish(0, 1, silu)
    gather_1 = ag_small(0, 1)
    rest_0 = ag_pass(0, 0, ag_0)
    rs_join(1, 0, rs_2)
    sum_first(1, 0)
    small_2 = rs_small(1, 0)
    arrived(gather_1)
    ag_1 = ag_big(0, 1)

    take(down_own.at[1], w_recv.at[3])
    partial(1, 1, dm, dt, down_own)
    rs_3 = rs_begin(1, 1)
    arrived(small_2)
    finish(1, 0, silu_back)
    gather_2 = ag_small(1, 0)
    rest_1 = ag_pass(0, 1, ag_1)
    settle(rest_0)
    rs_join(1, 1, rs_3)
    sum_first(1, 1)
    small_3 = rs_small(1, 1)
    arrived(gather_2)
    ag_2 = ag_big(1, 0)
    back_early(0, down_own)
    settle(rest_1)
    back_tail(0, down_own)
    near_0 = fold_near(0, down_own)
    arrived(small_3)
    finish(1, 1, silu_back)
    gather_3 = ag_small(1, 1)
    rest_2 = ag_pass(1, 0, ag_2)
    far_0 = fold_far(0, near_0)
    arrived(gather_3)
    ag_3 = ag_big(1, 1)
    arrived(far_0)
    give_back(0, y_out)
    rest_3 = ag_pass(1, 1, ag_3)
    settle(rest_2)
    back_early(1, up_own)
    gradient(dm, dt, 0, 0, gd_out)
    gradient(dm, dt, 0, 1, gd_out)
    settle(rest_3)
    back_tail(1, up_own)
    near_1 = fold_near(1, up_own)
    far_1 = fold_far(1, near_1)
    arrived(far_1)
    give_back(1, dx_out)
    gradient(xm, xt, 1, 0, gu_out)
    gradient(xm, xt, 1, 1, gu_out)
    take(y_out, o_recv.at[0])
    take(dx_out, o_recv.at[1])
    for c in started:
        c.wait_send()
    for t, own in enumerate((up_own, down_own)):
        for u in range(PARTS):
            take(own.at[u, pl.ds(0, n_dp - 1)], w_send.at[t * PARTS + u])
    for n, got in enumerate((x_got, d_got)):
        take(got.at[0, pl.ds(0, blocks - 1)], t_send.at[n])
    for n, got in enumerate((y_out, dx_out)):
        take(got.at[pl.ds(0, blocks - 1)], o_send.at[n])


def layer(x_msg, d_msg, up, down):
    n_dp = lax.axis_size("dp")
    own_f = x_msg.shape[2]
    rows = up.shape[1]
    quarters = n_dp // E
    blocks = n_dp // quarters
    hid = up.shape[2] // quarters
    hw = hid // PARTS
    main = n_dp * HEAD
    tails = blocks * TAIL
    wide = -(-hid // (SIDE * SIDE * 128)) * SIDE * SIDE * 128
    big = main // 2 // SIDE
    small = big // SIDE
    ht = tails // 2
    vm = pltpu.VMEM
    dma = pltpu.SemaphoreType.DMA
    return pl.pallas_call(
        layer_kernel,
        name="layer",
        out_shape=(
            jax.ShapeDtypeStruct((E, MSG, own_f), BF),
            jax.ShapeDtypeStruct((E, MSG, own_f), BF),
            jax.ShapeDtypeStruct((own_f, hid), BF),
            jax.ShapeDtypeStruct((own_f, hid), BF),
        ),
        in_specs=[pl.BlockSpec(memory_space=pltpu.VMEM)] * 2 + [pl.BlockSpec(memory_space=pl.ANY)] * 2,
        out_specs=[pl.BlockSpec(memory_space=pltpu.VMEM)] * 4,
        scratch_shapes=[
            vm((PARTS, n_dp, rows, hw), BF), vm((PARTS, n_dp, rows, hw), BF),
            vm((quarters, blocks, MSG, own_f), BF), vm((quarters, blocks, MSG, own_f), BF),
            vm((2, quarters, blocks, MSG, own_f), BF), vm((2, 2, blocks, MSG, own_f), BF),
            vm((2, blocks, MSG, own_f), BF),
            vm((main, own_f), BF), vm((tails, own_f), BF),
            vm((main, own_f), BF), vm((tails, own_f), BF),
            vm((tails, own_f), F32), vm((main, own_f), F32),
            vm((2, PARTS, main, hw), BF), vm((2, tails, wide), BF),
            vm((2, PARTS, 2, 2, big // 2, hw), BF), vm((2, 2, 2, ht // 2, wide // SIDE), BF),
            vm((2, PARTS, 2, 2, 2, big // 2, hw), BF), vm((2, 2, 2, 2, ht // 2, wide // SIDE), BF),
            vm((2, PARTS, 2, big, hw), BF), vm((2, 2, ht, wide // SIDE), BF),
            vm((2, PARTS, 2, SIDE - 1, small, hw), BF), vm((2, 2, SIDE - 1, ht, wide // SIDE // SIDE), BF),
            vm((PARTS, 2, small, hw), F32), vm((2, ht, wide // SIDE // SIDE), F32),
            vm((2, PARTS, main, hw), BF), vm((2, tails, wide), BF),
            dma((2 * PARTS,)), dma((2 * PARTS,)), dma((2,)), dma((2,)),
            dma((2, 3)), dma((2, 3)), dma((2, 3)), dma((2, 3)), dma((2,)), dma((2,)),
            dma((2 * PARTS, 2, 6, 2)), dma((2 * PARTS, 2, 6, 2)),
            dma((2 * PARTS, 2, SIDE - 1, 2)), dma((2 * PARTS, 2, SIDE - 1, 2)),
            dma((2 * PARTS, 2, SIDE - 1, 2)), dma((2 * PARTS, 2, SIDE - 1, 2)),
            dma((2 * PARTS, 2, 6, 2)), dma((2 * PARTS, 2, 6, 2)),
        ],
        compiler_params=pltpu.CompilerParams(
            collective_id=0, has_side_effects=True, vmem_limit_bytes=58 * 2**20
        ),
    )(x_msg, d_msg, up, down)


def body(tokens, routes, route_weights, up_stacked, down_stacked, cotangent):
    experts = jnp.arange(E, dtype=jnp.int32)
    named = routes[:, :, None] == experts[None, None, :]
    chosen = jnp.sum(named.astype(F32), axis=1)
    rows = jnp.arange(routes.shape[0], dtype=jnp.int32)
    earlier = (rows[None, :] < rows[:, None]).astype(BF)
    before = jnp.dot(earlier, chosen.astype(BF), preferred_element_type=F32).astype(jnp.int32)
    slot_pos = jnp.sum(jnp.where(named, before[:, None, :], 0), axis=2)
    shift = 2 * lax.rem(lax.axis_index("dp"), 4)
    target = routes * MSG + slot_pos + jnp.where(slot_pos >= HEAD, shift, 0)
    slot_hits = jnp.arange(E * MSG, dtype=jnp.int32)[:, None, None] == target[None, :, :]
    pick_table = jnp.sum(slot_hits.astype(F32), axis=2)
    weighted = jnp.sum(jnp.where(slot_hits, route_weights[None, :, :], 0.0), axis=2)
    features = tokens.shape[1]
    x_msg = jnp.dot(pick_table.astype(BF), tokens, preferred_element_type=F32).astype(BF)
    d_msg = jnp.dot(weighted, cotangent.astype(F32), precision=lax.Precision.HIGHEST).astype(BF)
    y_slots, dx_slots, g_up, g_down = layer(
        x_msg.reshape(E, MSG, features), d_msg.reshape(E, MSG, features), up_stacked, down_stacked
    )
    y_slots = y_slots.reshape(E * MSG, features).astype(F32)
    dx_slots = dx_slots.reshape(E * MSG, features).astype(F32)
    mixed = jnp.dot(weighted.T, y_slots, precision=lax.Precision.HIGHEST).astype(BF)
    grad_tokens = jnp.dot(pick_table.T, dx_slots, precision=lax.Precision.HIGHEST).astype(BF)
    return (mixed, grad_tokens, g_up[None], g_down[None])


def solution(mesh):
    placed = (
        P("dp", "member"),
        P("dp", None),
        P("dp", None),
        P(None, ("member", "dp"), None),
        P(None, ("member", "dp"), None),
        P("dp", "member"),
    )
    return jax.shard_map(
        body,
        mesh=mesh,
        in_specs=placed,
        out_specs=(
            P("dp", "member"),
            P("dp", "member"),
            P("dp", "member", None),
            P("dp", "member", None),
        ),
        check_vma=False,
    )
```

time: 232 us -> 216 us (0.931)
  Pallas kernels: 222 us -> 205 us
    pallas_call x1, Pallas kernels: 222 us -> 205 us  [layer(): pl.pallas_call(layer_kernel, name='layer', out_shape=(jax.ShapeDtypeStruc...]
where the time goes in v4:
time: 216 us; the launch traced here: 215 us
  Pallas kernels  205 us (95%)
  matrix products  4.87 us (2%)
  local copies, waits for them, and re-layouts  4.55 us (2%)
    pallas_call x1, Pallas kernels, layer(): pl.pallas_call(layer_kernel, name='layer', out_shape=(jax.ShapeDtypeStruc...  205 us
    unnamed x14, local copies, waits for them, and re-layouts  4.55 us

profile of v4, /device:TPU:1, one launch (start us, length us, event | category | flops | bytes accessed | tf_op | source)
XLA Modules:
  0.0 215.5 jit_solution(3050170484552714146)
XLA Ops:
  0.6 0.0 copy-start
  0.7 0.0 copy-start.4
  0.7 0.7 copy-done.4
  1.4 0.1 convolution_convert_fusion.4
  1.5 0.0 copy-start.5
  1.6 0.7 copy-done.5
  2.2 0.1 convert_reduce_fusion
  2.3 0.0 copy-done
  2.3 0.0 copy-start.3
  2.3 0.9 convolution_convert_fusion.1
  3.2 0.0 copy-done.3
  3.2 0.9 convolution_convert_fusion
  4.1 205.2 %layer.1 = (bf16[8,40,256]{2,1,0:T(8,128)(2,1)}, bf16[8,40,256]{2,1,0:T(8,128)(2,1)}, bf16[256,1792]{1,0:T(8,128)(2,1)}, bf16[256,1792]{1,0:T(8,128)(2,1)}) custom-call(bf16[8,40,256]{2,1,0:T(8,128)(2,1)} %bitcast.16, bf16[8,40,256]{2,1,0:T(8,128)(2,1)} %bitcast.17, bf16[8,8,7168]{2,1,0:T(8,128)(2,1)} %up.1, bf16[8,8,7168]{2,1,0:T(8,128)(2,1)} %down.1), custom_call_target="tpu_custom_call" | custom-call | tf_op jit(solution)/shard_map/layer/pallas_call | solution.py:538
  209.3 0.0 copy-start.2
  209.4 1.9 convolution_convert_fusion.3
  211.3 0.0 copy-done.2
  211.3 1.0 convolution_convert_fusion.2
  212.3 0.0 copy-start.1
  212.3 2.2 %copy.16 = bf16[1,256,1792]{2,1,0:T(8,128)(2,1)} copy(bf16[1,256,1792]{2,1,0:T(8,128)(2,1)} %bitcast.15) | data formatting | bytes 1835008
  214.5 0.0 copy-done.1
  214.5 0.9 copy.17
  (3 shorter events, 0.0 us)
Async XLA Ops:
  0.6 1.7 copy-start
  0.7 0.7 copy-start.4
  1.5 0.7 copy-start.5
  2.3 0.9 copy-start.3
  209.3 2.0 copy-start.2
  212.3 2.2 %copy-start.1 = (bf16[256,1792]{1,0:T(8,128)(2,1)S(1)}, bf16[256,1792]{1,0:T(8,128)(2,1)}, u32[]{:S(2)}) copy-start(bf16[256,1792]{1,0:T(8,128)(2,1)} %get-tuple-element.11) | copy-start | bytes 2752516

commit v5 on v4

--- a/solution.py
+++ b/solution.py
@@ -26,8 +26,9 @@
 
 
 def layer_kernel(
-    x_msg, d_msg, up, down,
-    y_out, dx_out, gu_out, gd_out,
+    x_msg, d_msg, weighted, pick, up, down,
+    mixed_out, gt_out, gu_out, gd_out,
+    y_got, dx_got,
     up_own, down_own, x_got, d_got, back_msg, sum_in, sum_far,
     xm, xt, dm, dt, tail32, early,
     pm, pt, ram, rat, rbm, rbt, sm, st, r2m, r2t, pre_m, pre_t, fm, ft,
@@ -97,6 +98,11 @@
         started.extend(copies)
         return copies
 
+    def drain(count):
+        for c in started[:count]:
+            c.wait_send()
+        del started[:count]
+
     def arrived(copies):
         for c in copies:
             c.wait_recv()
@@ -404,6 +410,9 @@
 
         pltpu.make_async_copy(back_msg.at[t, q, e], got.at[e], o_recv.at[t]).start()
 
+    def returned(got):
+        return got[...].astype(F32).reshape(E * MSG, own_f)
+
     def gradient(main, tail, t, u, out):
         @pl.loop(0, hw // 128)
         def _(c):
@@ -413,12 +422,12 @@
             out[:, pl.ds(u * hw + at, 128)] = g.astype(BF)
 
     send_tokens(0, x_msg, x_got)
-    send_weights(0, 0, up, up_own, 0, 8)
+    send_weights(0, 0, up, up_own, 0, 20)
     keep_weights(0, up, up_own)
     keep_weights(1, down, down_own)
     take(x_got.at[q], t_recv.at[0])
     xf = relay_far(0, x_got)
-    send_weights(0, 0, up, up_own, 8, n_dp - 1)
+    send_weights(0, 0, up, up_own, 20, n_dp - 1)
     arrived(xf)
     xn = relay_near(0, x_got)
     send_weights(0, 1, up, up_own, 0, n_dp - 1)
@@ -469,6 +478,7 @@
 
     take(down_own.at[1], w_recv.at[3])
     partial(1, 1, dm, dt, down_own)
+    before_3 = len(started)
     rs_3 = rs_begin(1, 1)
     arrived(small_2)
     finish(1, 0, silu_back)
@@ -489,10 +499,11 @@
     gather_3 = ag_small(1, 1)
     rest_2 = ag_pass(1, 0, ag_2)
     far_0 = fold_far(0, near_0)
+    drain(before_3)
     arrived(gather_3)
     ag_3 = ag_big(1, 1)
     arrived(far_0)
-    give_back(0, y_out)
+    give_back(0, y_got)
     rest_3 = ag_pass(1, 1, ag_3)
     settle(rest_2)
     back_early(1, up_own)
@@ -503,23 +514,27 @@
     near_1 = fold_near(1, up_own)
     far_1 = fold_far(1, near_1)
     arrived(far_1)
-    give_back(1, dx_out)
+    give_back(1, dx_got)
     gradient(xm, xt, 1, 0, gu_out)
     gradient(xm, xt, 1, 1, gu_out)
-    take(y_out, o_recv.at[0])
-    take(dx_out, o_recv.at[1])
-    for c in started:
-        c.wait_send()
+    take(y_got, o_recv.at[0])
+    mixed_out[...] = lax.dot_general(
+        weighted[...], returned(y_got), (((0,), (0,)), ((), ())),
+        precision=lax.Precision.HIGHEST, preferred_element_type=F32,
+    ).astype(BF)
+    drain(len(started))
     for t, own in enumerate((up_own, down_own)):
         for u in range(PARTS):
             take(own.at[u, pl.ds(0, n_dp - 1)], w_send.at[t * PARTS + u])
     for n, got in enumerate((x_got, d_got)):
         take(got.at[0, pl.ds(0, blocks - 1)], t_send.at[n])
-    for n, got in enumerate((y_out, dx_out)):
+    take(dx_got, o_recv.at[1])
+    gt_out[...] = dot(pick[...], returned(dx_got).astype(BF), 0, 0).astype(BF)
+    for n, got in enumerate((y_got, dx_got)):
         take(got.at[pl.ds(0, blocks - 1)], o_send.at[n])
 
 
-def layer(x_msg, d_msg, up, down):
+def layer(x_msg, d_msg, weighted, pick, up, down):
     n_dp = lax.axis_size("dp")
     own_f = x_msg.shape[2]
     rows = up.shape[1]
@@ -539,14 +554,15 @@
         layer_kernel,
         name="layer",
         out_shape=(
-            jax.ShapeDtypeStruct((E, MSG, own_f), BF),
-            jax.ShapeDtypeStruct((E, MSG, own_f), BF),
+            jax.ShapeDtypeStruct((weighted.shape[1], own_f), BF),
+            jax.ShapeDtypeStruct((weighted.shape[1], own_f), BF),
             jax.ShapeDtypeStruct((own_f, hid), BF),
             jax.ShapeDtypeStruct((own_f, hid), BF),
         ),
-        in_specs=[pl.BlockSpec(memory_space=pltpu.VMEM)] * 2 + [pl.BlockSpec(memory_space=pl.ANY)] * 2,
+        in_specs=[pl.BlockSpec(memory_space=pltpu.VMEM)] * 4 + [pl.BlockSpec(memory_space=pl.ANY)] * 2,
         out_specs=[pl.BlockSpec(memory_space=pltpu.VMEM)] * 4,
         scratch_shapes=[
+            vm((E, MSG, own_f), BF), vm((E, MSG, own_f), BF),
             vm((PARTS, n_dp, rows, hw), BF), vm((PARTS, n_dp, rows, hw), BF),
             vm((quarters, blocks, MSG, own_f), BF), vm((quarters, blocks, MSG, own_f), BF),
             vm((2, quarters, blocks, MSG, own_f), BF), vm((2, 2, blocks, MSG, own_f), BF),
@@ -571,7 +587,7 @@
         compiler_params=pltpu.CompilerParams(
             collective_id=0, has_side_effects=True, vmem_limit_bytes=58 * 2**20
         ),
-    )(x_msg, d_msg, up, down)
+    )(x_msg, d_msg, weighted, pick, up, down)
 
 
 def body(tokens, routes, route_weights, up_stacked, down_stacked, cotangent):
@@ -590,13 +606,10 @@
     features = tokens.shape[1]
     x_msg = jnp.dot(pick_table.astype(BF), tokens, preferred_element_type=F32).astype(BF)
     d_msg = jnp.dot(weighted, cotangent.astype(F32), precision=lax.Precision.HIGHEST).astype(BF)
-    y_slots, dx_slots, g_up, g_down = layer(
-        x_msg.reshape(E, MSG, features), d_msg.reshape(E, MSG, features), up_stacked, down_stacked
+    mixed, grad_tokens, g_up, g_down = layer(
+        x_msg.reshape(E, MSG, features), d_msg.reshape(E, MSG, features), weighted, pick_table.astype(BF),
+        up_stacked, down_stacked,
     )
-    y_slots = y_slots.reshape(E * MSG, features).astype(F32)
-    dx_slots = dx_slots.reshape(E * MSG, features).astype(F32)
-    mixed = jnp.dot(weighted.T, y_slots, precision=lax.Precision.HIGHEST).astype(BF)
-    grad_tokens = jnp.dot(pick_table.T, dx_slots, precision=lax.Precision.HIGHEST).astype(BF)
     return (mixed, grad_tokens, g_up[None], g_down[None])
 
 

time: 216 us -> 213 us (0.986)
  matrix products: 4.87 us -> 1.94 us
    dot_general x2 -> x0, matrix products: 2.93 us -> none  [the longest x1 1.94 us: body(): jnp.dot(weighted.T, y_slots, precision=lax.Precision.HIGHEST).astype(BF)]
    unnamed x14 -> x20, local copies, waits for them, and re-layouts: 4.55 us -> 6.7 us
where the time goes in v5:
time: 213 us
  Pallas kernels  203 us (95%)
  local copies, waits for them, and re-layouts  6.7 us (3%)
    pallas_call x1, Pallas kernels, layer(): pl.pallas_call(layer_kernel, name='layer', out_shape=(jax.ShapeDtypeStruc...  203 us
    unnamed x20, local copies, waits for them, and re-layouts  6.7 us

profile of v5, /device:TPU:1, one launch (start us, length us, event | category | flops | bytes accessed | tf_op | source)
XLA Modules:
  0.0 212.6 jit_solution(10979930124094666672)
XLA Ops:
  0.6 0.0 copy-start
  0.7 0.0 copy-start.6
  0.7 0.7 copy-done.6
  1.4 0.1 convolution_convert_fusion.2
  1.5 0.0 copy-start.7
  1.6 0.7 copy-done.7
  2.2 0.1 select_reduce_fusion
  2.3 0.0 copy-start.1
  2.3 0.0 copy-start.3
  2.3 0.0 copy-done
  2.3 0.0 copy-start.4
  2.3 0.9 convolution_convert_fusion
  3.3 0.0 copy-done.1
  3.3 0.0 copy-done.3
  3.3 0.0 copy-done.4
  3.3 0.9 convolution_convert_fusion.1
  4.1 203.1 %layer.1 = (bf16[128,256]{1,0:T(8,128)(2,1)}, bf16[128,256]{1,0:T(8,128)(2,1)}, bf16[256,1792]{1,0:T(8,128)(2,1)}, bf16[256,1792]{1,0:T(8,128)(2,1)}) custom-call(bf16[8,40,256]{2,1,0:T(8,128)(2,1)} %bitcast.12, bf16[8,40,256]{2,1,0:T(8,128)(2,1)} %bitcast.11, f32[320,128]{1,0:T(8,128)} %copy-done.1, bf16[320,128]{1,0:T(8,128)(2,1)} %copy-done.3, ...), custom_call_target="tpu_custom_call" | custom-call | tf_op jit(solution)/shard_map/layer/pallas_call | solution.py:553
  207.2 0.0 copy-start.5
  207.3 1.5 copy.18
  208.8 0.0 copy-done.5
  208.8 0.6 copy.19
  209.4 0.0 copy-start.2
  209.4 2.2 %copy.20 = bf16[1,256,1792]{2,1,0:T(8,128)(2,1)} copy(bf16[1,256,1792]{2,1,0:T(8,128)(2,1)} %bitcast.10) | data formatting | bytes 1835008
  211.6 0.0 copy-done.2
  211.6 0.9 copy.21
  (3 shorter events, 0.0 us)
Async XLA Ops:
  0.6 1.7 copy-start
  0.7 0.7 copy-start.6
  1.5 0.7 copy-start.7
  2.3 1.0 copy-start.1
  2.3 1.0 copy-start.3
  2.3 1.0 copy-start.4
  207.2 1.5 copy-start.5
  209.4 2.2 %copy-start.2 = (bf16[256,1792]{1,0:T(8,128)(2,1)S(1)}, bf16[256,1792]{1,0:T(8,128)(2,1)}, u32[]{:S(2)}) copy-start(bf16[256,1792]{1,0:T(8,128)(2,1)} %get-tuple-element.11) | copy-start | bytes 2752516

commit v6 on v5

--- a/solution.py
+++ b/solution.py
@@ -26,9 +26,9 @@
 
 
 def layer_kernel(
-    x_msg, d_msg, weighted, pick, up, down,
+    tokens, cotangent, weighted, pick, up, down,
     mixed_out, gt_out, gu_out, gd_out,
-    y_got, dx_got,
+    x_msg, d_msg, y_got, dx_got,
     up_own, down_own, x_got, d_got, back_msg, sum_in, sum_far,
     xm, xt, dm, dt, tail32, early,
     pm, pt, ram, rat, rbm, rbt, sm, st, r2m, r2t, pre_m, pre_t, fm, ft,
@@ -85,6 +85,13 @@
     for k in range(1, SIDE):
         pl.semaphore_signal(barrier, inc=1, device_id=peer_first(0, k)[1])
         pl.semaphore_signal(barrier, inc=1, device_id=peer_first(1, k)[1])
+    rows = dot(pick[...], tokens[...], 1, 0)
+    x_msg[...] = rows.reshape(E, MSG, own_f).astype(BF)
+    rows = lax.dot_general(
+        weighted[...], cotangent[...].astype(F32), (((1,), (0,)), ((), ())),
+        precision=lax.Precision.HIGHEST, preferred_element_type=F32,
+    )
+    d_msg[...] = rows.reshape(E, MSG, own_f).astype(BF)
     pl.semaphore_wait(barrier, n_dp - 1 + 2 * (SIDE - 1))
 
     def remote(src, dst, send, recv, dev):
@@ -465,6 +472,7 @@
 
     take(down_own.at[0], w_recv.at[2])
     partial(1, 0, dm, dt, down_own)
+    before_2 = len(started)
     rs_2 = rs_begin(1, 0)
     arrived(small_1)
     finish(0, 1, silu)
@@ -499,7 +507,7 @@
     gather_3 = ag_small(1, 1)
     rest_2 = ag_pass(1, 0, ag_2)
     far_0 = fold_far(0, near_0)
-    drain(before_3)
+    drain(before_2)
     arrived(gather_3)
     ag_3 = ag_big(1, 1)
     arrived(far_0)
@@ -508,13 +516,14 @@
     settle(rest_2)
     back_early(1, up_own)
     gradient(dm, dt, 0, 0, gd_out)
-    gradient(dm, dt, 0, 1, gd_out)
+    drain(before_3 - before_2)
     settle(rest_3)
     back_tail(1, up_own)
     near_1 = fold_near(1, up_own)
     far_1 = fold_far(1, near_1)
     arrived(far_1)
     give_back(1, dx_got)
+    gradient(dm, dt, 0, 1, gd_out)
     gradient(xm, xt, 1, 0, gu_out)
     gradient(xm, xt, 1, 1, gu_out)
     take(y_got, o_recv.at[0])
@@ -534,9 +543,9 @@
         take(got.at[pl.ds(0, blocks - 1)], o_send.at[n])
 
 
-def layer(x_msg, d_msg, weighted, pick, up, down):
+def layer(tokens, cotangent, weighted, pick, up, down):
     n_dp = lax.axis_size("dp")
-    own_f = x_msg.shape[2]
+    own_f = tokens.shape[1]
     rows = up.shape[1]
     quarters = n_dp // E
     blocks = n_dp // quarters
@@ -563,6 +572,7 @@
         out_specs=[pl.BlockSpec(memory_space=pltpu.VMEM)] * 4,
         scratch_shapes=[
             vm((E, MSG, own_f), BF), vm((E, MSG, own_f), BF),
+            vm((E, MSG, own_f), BF), vm((E, MSG, own_f), BF),
             vm((PARTS, n_dp, rows, hw), BF), vm((PARTS, n_dp, rows, hw), BF),
             vm((quarters, blocks, MSG, own_f), BF), vm((quarters, blocks, MSG, own_f), BF),
             vm((2, quarters, blocks, MSG, own_f), BF), vm((2, 2, blocks, MSG, own_f), BF),
@@ -587,7 +597,7 @@
         compiler_params=pltpu.CompilerParams(
             collective_id=0, has_side_effects=True, vmem_limit_bytes=58 * 2**20
         ),
-    )(x_msg, d_msg, weighted, pick, up, down)
+    )(tokens, cotangent, weighted, pick, up, down)
 
 
 def body(tokens, routes, route_weights, up_stacked, down_stacked, cotangent):
@@ -603,12 +613,8 @@
     slot_hits = jnp.arange(E * MSG, dtype=jnp.int32)[:, None, None] == target[None, :, :]
     pick_table = jnp.sum(slot_hits.astype(F32), axis=2)
     weighted = jnp.sum(jnp.where(slot_hits, route_weights[None, :, :], 0.0), axis=2)
-    features = tokens.shape[1]
-    x_msg = jnp.dot(pick_table.astype(BF), tokens, preferred_element_type=F32).astype(BF)
-    d_msg = jnp.dot(weighted, cotangent.astype(F32), precision=lax.Precision.HIGHEST).astype(BF)
     mixed, grad_tokens, g_up, g_down = layer(
-        x_msg.reshape(E, MSG, features), d_msg.reshape(E, MSG, features), weighted, pick_table.astype(BF),
-        up_stacked, down_stacked,
+        tokens, cotangent, weighted, pick_table.astype(BF), up_stacked, down_stacked
     )
     return (mixed, grad_tokens, g_up[None], g_down[None])
 

time: 213 us -> 210 us (0.986); the launches traced: 213 us -> 206 us
  Pallas kernels: 203 us -> 198 us
    pallas_call x1, Pallas kernels: 203 us -> 198 us  [layer(): pl.pallas_call(layer_kernel, name='layer', out_shape=(jax.ShapeDtypeStruc...]
    unnamed x20 -> x12, local copies, waits for them, and re-layouts: 6.7 us -> 6.64 us
where the time goes in v6:
time: 210 us; the launch traced here: 206 us
  Pallas kernels  198 us (94%)
  local copies, waits for them, and re-layouts  6.64 us (3%)
    pallas_call x1, Pallas kernels, layer(): pl.pallas_call(layer_kernel, name='layer', out_shape=(jax.ShapeDtypeStruc...  198 us
    unnamed x12, local copies, waits for them, and re-layouts  6.64 us

profile of v6, /device:TPU:1, one launch (start us, length us, event | category | flops | bytes accessed | tf_op | source)
XLA Modules:
  0.0 206.2 jit_solution(10103052525282138795)
XLA Ops:
  0.6 0.0 copy-start.2
  0.6 0.7 copy-done.2
  1.3 0.1 convolution_convert_fusion
  1.5 0.0 copy-start.3
  1.5 0.7 copy-done.3
  2.2 0.8 convert_reduce_fusion
  2.9 197.9 %layer.1 = (bf16[128,256]{1,0:T(8,128)(2,1)}, bf16[128,256]{1,0:T(8,128)(2,1)}, bf16[256,1792]{1,0:T(8,128)(2,1)}, bf16[256,1792]{1,0:T(8,128)(2,1)}) custom-call(bf16[128,256]{1,0:T(8,128)(2,1)} %tokens.1, bf16[128,256]{1,0:T(8,128)(2,1)} %cotangent.1, f32[320,128]{1,0:T(8,128)} %get-tuple-element.13.weighted, bf16[320,128]{1,0:T(8,128)(2,1)} %get-tuple-element.12.pick, ...), custom_call_target="tpu_custom_call" | custom-call | tf_op jit(solution)/shard_map/layer/pallas_call | solution.py:562
  200.8 0.0 copy-start.1
  200.9 1.5 copy.18
  202.4 0.0 copy-done.1
  202.4 0.6 copy.19
  203.0 0.0 copy-start
  203.0 2.2 %copy.20 = bf16[1,256,1792]{2,1,0:T(8,128)(2,1)} copy(bf16[1,256,1792]{2,1,0:T(8,128)(2,1)} %bitcast.4) | data formatting | bytes 1835008
  205.2 0.0 copy-done
  205.2 0.9 copy.21
  (3 shorter events, 0.0 us)
Async XLA Ops:
  0.6 0.7 copy-start.2
  1.5 0.7 copy-start.3
  200.8 1.5 copy-start.1
  203.0 2.2 %copy-start = (bf16[256,1792]{1,0:T(8,128)(2,1)S(1)}, bf16[256,1792]{1,0:T(8,128)(2,1)}, u32[]{:S(2)}) copy-start(bf16[256,1792]{1,0:T(8,128)(2,1)} %get-tuple-element.11) | copy-start | bytes 2752516
